TPU v7x, 128 devices: a whole 4x4x4 slice. The times are simulated.
128 devices in a mesh: expert: 8 (over z, core), fsdp: 16 (over y, x).
Axes of the slice: x: 4, y: 4, z: 4, core: 2. Of those that a mesh axis runs over, the one named last changes fastest.
Arguments:
- tokens: bfloat16 [32768, 2048], P(('expert', 'fsdp')), may hold values from -6 to 6
- expert_ids: int32 [32768, 6], P(('expert', 'fsdp')), may hold values from 0 to 63, as said below
- gate_vals: bfloat16 [32768, 6], P(('expert', 'fsdp')), may hold values from 0.099609375 to 1
- w_gate: bfloat16 [8, 2048, 1408], P('expert', 'fsdp'), may hold values from -0.125 to 0.125
- w_up: bfloat16 [8, 2048, 1408], P('expert', 'fsdp'), may hold values from -0.125 to 0.125
- w_down: bfloat16 [8, 2048, 1408], P('expert', 'fsdp'), may hold values from -0.15625 to 0.15625
- cotangent: bfloat16 [32768, 2048], P(('expert', 'fsdp')), may hold values from -6 to 6
Outputs:
- output: bfloat16 [32768, 2048], P(('expert', 'fsdp'))
- grad_tokens: bfloat16 [32768, 2048], P(('expert', 'fsdp'))
- grad_gates: float32 [32768, 6], P(('expert', 'fsdp'))
- grad_w_gate: float32 [8, 2048, 1408], P('expert', 'fsdp')
- grad_w_up: float32 [8, 2048, 1408], P('expert', 'fsdp')
- grad_w_down: float32 [8, 2048, 1408], P('expert', 'fsdp')
Inputs may be any that keep to these rules, and one draw needn't show every extreme that they name: `expert_ids`: each row names 6 different experts. Among the tokens of one device at most 48 name any one expert whose number modulo 8 is below 1. On every device some such expert is named by exactly 48 of its tokens, and for every column one such expert is named by exactly 48 tokens of every device of that column.
All inputs are finite; a program needn't handle non-finite values.
Results may differ from a plain program's by a relative error of at most 0.013.
Values may be sent and summed in bfloat16 or wider, within the bound.
No kernel may reach another device: no remote copies, remote signals or barrier semaphores. Data moves between devices by JAX's collectives and lax.ppermute only.
A program may use at most 128 MiB of HBM per device.

v0:
```python
import functools

import jax
import jax.numpy as jnp
from jax import lax
from jax.experimental import pallas as pl
from jax.experimental.pallas import tpu as pltpu
from jax.sharding import PartitionSpec as P

TOP = 6
MOST = 48
OWNED = 8
LANE = 128
AXES = ("expert", "fsdp")
F32 = jnp.float32
BF16 = jnp.bfloat16


def pairs_of(move):
    pairs = []
    for source in range(128):
        z, core, y, x = source // 32, source // 16 % 2, source // 4 % 4, source % 4
        core, y, x = move(core, y, x)
        pairs.append((source, (z * 2 + core) * 16 + y % 4 * 4 + x))
    return pairs


TO_CORE = pairs_of(lambda core, y, x: (1 - core, y, x))
TO_MIRROR = pairs_of(lambda core, y, x: (core, y, 3 - x))
TO_SIDE = pairs_of(lambda core, y, x: (core, y, x ^ 1))
TO_UP = pairs_of(lambda core, y, x: (core, y + 1, x))
TO_DOWN = pairs_of(lambda core, y, x: (core, y - 1, x))
Z_GROUPS = [[0, 2, 4, 6], [1, 3, 5, 7]]


MOVES = {"core": TO_CORE, "mirror": TO_MIRROR, "side": TO_SIDE, "up": TO_UP, "down": TO_DOWN, "rows": TO_MIRROR}


def after(value, *others):
    return lax.optimization_barrier((value,) + others)[0]


class Rounds:
    def __init__(self):
        self.number, self.held, self.ended, self.ready = 0, [], (), []

    def hold(self, value, rounds=1):
        self.held.append((self.number + rounds, value))
        return value

    def pin(self, value):
        return after(value, *self.ended) if self.ended else value

    def late(self, value):
        return after(value, *self.ready)

    def send(self, link, value, rounds=1):
        value = self.pin(value)
        self.ready.append(value)
        return self.hold(lax.ppermute(value, AXES, MOVES[link]), rounds)

    def exchange(self, value, rounds=1):
        moved = lax.all_to_all(
            value,
            "expert",
            split_axis=0,
            concat_axis=0,
            tiled=True,
            axis_index_groups=Z_GROUPS,
        )
        return self.hold(moved, rounds)

    def next(self):
        self.number += 1
        self.ready = []
        self.ended = tuple(v for due, v in self.held if due == self.number)


def routes(ids, half, own):
    tok_count = ids.shape[1]
    side = half if own else 1 - half
    live = []
    for z in range(4):
        wanted = OWNED * (2 * z + side)
        live.append(jnp.sum(jnp.where(ids == wanted, 1.0, 0.0), axis=0, keepdims=True))
    live = jnp.concatenate(live + [jnp.zeros((4, tok_count), F32)], axis=0)
    before = lax.broadcasted_iota(jnp.int32, (tok_count, tok_count), 0)
    after = lax.broadcasted_iota(jnp.int32, (tok_count, tok_count), 1)
    earlier = jnp.where(before < after, 1.0, 0.0).astype(BF16)
    rank = jnp.dot(live.astype(BF16), earlier, preferred_element_type=F32)
    row = lax.broadcasted_iota(jnp.int32, (MOST, tok_count), 0).astype(F32)
    chosen = []
    for z in range(4):
        here = jnp.where(row == rank[z : z + 1], 1.0, 0.0) * live[z : z + 1]
        chosen.append(here)
    return chosen


def gates_of(ids, gates, half, own):
    side = half if own else 1 - half
    return [
        jnp.sum(jnp.where(ids == OWNED * (2 * z + side), gates, 0.0), axis=0, keepdims=True)
        for z in range(4)
    ]


def dispatch_kernel(place, ids_ref, gates_ref, tok_ref, cot_ref, *outs):
    y, half = place[0], place[1]
    ids = ids_ref[...]
    gates = gates_ref[...].astype(F32)
    width = tok_ref.shape[1] // 8
    for own in (True, False):
        chosen = routes(ids, half, own)
        gate = gates_of(ids, gates, half, own)
        weight = jnp.concatenate(
            [jnp.sum(s * g, axis=1, keepdims=True) for s, g in zip(chosen, gate)], axis=0
        )
        select = jnp.concatenate(chosen, axis=0).astype(BF16)
        side = half if own else 1 - half
        for kind in range(2):
            for step in range(4):
                block = lax.rem(y + step, 4) * 2 + (side if kind == 0 else 1 - side)
                read = pl.ds(pl.multiple_of(block * width, width), width)
                put = slice((kind * 4 + step) * width, (kind * 4 + step + 1) * width)
                rows = jnp.dot(select, tok_ref[:, read], preferred_element_type=F32).astype(BF16)
                cots = jnp.dot(select, cot_ref[:, read], preferred_element_type=F32)
                grads = (weight * cots).astype(BF16)
                if own:
                    for z in range(4):
                        at, part = 2 * z * MOST, slice(z * MOST, (z + 1) * MOST)
                        outs[0][at : at + MOST, put] = rows[part]
                        outs[0][at + MOST : at + 2 * MOST, put] = grads[part]
                else:
                    outs[1][:, put] = rows
                    outs[2][:, put] = grads


def dispatch(place, ids, gates, tokens, cotangent):
    width = tokens.shape[1]
    both = jax.ShapeDtypeStruct((8 * MOST, width), BF16)
    rows = jax.ShapeDtypeStruct((4 * MOST, width), BF16)
    whole = pl.BlockSpec(memory_space=pltpu.VMEM)
    return pl.pallas_call(
        dispatch_kernel,
        out_shape=(both, rows, rows),
        in_specs=[pl.BlockSpec(memory_space=pltpu.SMEM)] + [whole] * 4,
        out_specs=(whole,) * 3,
        compiler_params=pltpu.CompilerParams(vmem_limit_bytes=48 << 20),
        cost_estimate=pl.CostEstimate(
            flops=1_000_000_000, bytes_accessed=6_000_000, transcendentals=0
        ),
        name="dispatch",
    )(place, ids, gates, tokens, cotangent)


TURNED = (((0,), (0,)), ((), ()))


def combine_kernel(
    place, ids_ref, gates_ref, cot_ref, own_ref, oth_ref, gown_ref, goth_ref, out_ref, gtok_ref, gg_ref
):
    y, half = place[0], place[1]
    ids = ids_ref[...]
    gates = gates_ref[...].astype(F32)
    width = cot_ref.shape[1] // 8
    picked, weighted, chosen_of = [], [], []
    for own in (True, False):
        chosen = routes(ids, half, own)
        gate = gates_of(ids, gates, half, own)
        picked.append(jnp.concatenate(chosen, axis=0).astype(BF16))
        weighted.append(
            jnp.concatenate([s * g for s, g in zip(chosen, gate)], axis=0).astype(BF16)
        )
        chosen_of.append(chosen)
    totals = [jnp.zeros((4 * MOST, 1), F32) for _ in range(2)]
    for step in range(4):
        for kind in range(2):
            block = lax.rem(y + step, 4) * 2 + (half if kind == 0 else 1 - half)
            at = pl.ds(pl.multiple_of(block * width, width), width)
            mine = slice((kind * 4 + step) * width, (kind * 4 + step + 1) * width)
            other = slice(((1 - kind) * 4 + step) * width, ((1 - kind) * 4 + step + 1) * width)
            cot = cot_ref[:, at]
            outs = (own_ref[:, mine], oth_ref[:, other])
            grads = (gown_ref[:, mine], goth_ref[:, other])
            out_ref[:, at] = sum(
                lax.dot_general(w, o, TURNED, preferred_element_type=F32)
                for w, o in zip(weighted, outs)
            ).astype(BF16)
            gtok_ref[:, at] = sum(
                lax.dot_general(s, g, TURNED, preferred_element_type=F32)
                for s, g in zip(picked, grads)
            ).astype(BF16)
            for i in range(2):
                cots = jnp.dot(picked[i], cot, preferred_element_type=F32)
                totals[i] += jnp.sum(cots * outs[i].astype(F32), axis=1, keepdims=True)
    result = jnp.zeros(ids.shape, F32)
    for i, own in enumerate((True, False)):
        side = half if own else 1 - half
        for z in range(4):
            per_slot = totals[i][z * MOST : (z + 1) * MOST]
            per_token = jnp.sum(chosen_of[i][z] * per_slot, axis=0, keepdims=True)
            result += jnp.where(ids == OWNED * (2 * z + side), per_token, 0.0)
    gg_ref[...] = result


def combine(place, ids, gates, cotangent, own, oth, gown, goth):
    shape = jax.ShapeDtypeStruct(cotangent.shape, BF16)
    whole = pl.BlockSpec(memory_space=pltpu.VMEM)
    return pl.pallas_call(
        combine_kernel,
        out_shape=(shape, shape, jax.ShapeDtypeStruct(ids.shape, F32)),
        in_specs=[pl.BlockSpec(memory_space=pltpu.SMEM)] + [whole] * 7,
        out_specs=(whole,) * 3,
        compiler_params=pltpu.CompilerParams(vmem_limit_bytes=48 << 20),
        cost_estimate=pl.CostEstimate(
            flops=2_000_000_000, bytes_accessed=8_000_000, transcendentals=0
        ),
        name="combine",
    )(place, ids, gates, cotangent, own, oth, gown, goth)


def half_width(width):
    return -(-width // (2 * LANE)) * LANE


def split_kernel(place, gate_hbm, up_hbm, down_hbm, keep_ref, give_ref, refs, sems):
    hbms = (gate_hbm, up_hbm, down_hbm)
    started = fetch([(hbm.at[0], refs.at[i]) for i, hbm in enumerate(hbms)], sems)
    part = keep_ref.shape[2]
    width = refs.shape[2]
    first = place[3] == 0
    for i, copy in enumerate(started):
        copy.wait()
        left = refs[i, :, :part]
        blank = jnp.zeros((left.shape[0], 2 * part - width), left.dtype)
        right = jnp.concatenate([blank, refs[i, :, part:]], axis=1)
        keep_ref[i] = jnp.where(first, left, right)
        give_ref[i] = jnp.where(first, right, left)


def choose_kernel(place, keep_ref, got_ref, own_gu, own_dn, away_gu, away_dn):
    here = place[3] == place[1]
    for i in range(3):
        own, away, at = (own_gu, away_gu, i) if i < 2 else (own_dn, away_dn, 0)
        own[at] = jnp.where(here, keep_ref[i], got_ref[i])
        away[at] = jnp.where(here, got_ref[i], keep_ref[i])


def in_pair(first, mine, theirs, axis):
    return jnp.where(
        first,
        jnp.concatenate([mine, theirs], axis=axis),
        jnp.concatenate([theirs, mine], axis=axis),
    )


def add(*terms):
    return sum(t.astype(F32) for t in terms).astype(BF16)


def whole_width(mine, other, width, core):
    part = mine.shape[2]
    left = jnp.where(core == 0, mine, other)
    right = jnp.where(core == 0, other, mine)
    return jnp.concatenate([left, right[:, :, 2 * part - width :]], axis=2).astype(F32)


def dot(a, b, over):
    return lax.dot_general(a, b, (over, ((), ())), preferred_element_type=F32)


WIDE = 256


def fetch(copies, sems):
    started = [pltpu.make_async_copy(a, b, sems.at[i]) for i, (a, b) in enumerate(copies)]
    for copy in started:
        copy.start()
    return started


def gate_up_pieces(low, refs, full):
    block0, block1, block2, block3, mir0, mir1, mir3, far, side_a, side_b = refs
    rows = mir0.shape[1]
    copies = [
        (block, full.at[:, pl.ds(2 * rows * i, 2 * rows), :])
        for i, block in enumerate((block0, block1, block2, block3))
    ]
    for i, (mine, theirs) in enumerate(
        (
            (mir0, side_a.at[0:2]),
            (mir1, side_a.at[2:4]),
            (far.at[0:2], side_b.at[2:4]),
            (mir3, side_b.at[0:2]),
        )
    ):
        start = (8 + 2 * i) * rows
        copies.append((mine, full.at[:, pl.ds(start + (1 - low) * rows, rows), :]))
        copies.append((theirs, full.at[:, pl.ds(start + low * rows, rows), :]))
    return copies


def down_pieces(low, refs, full):
    own0, own1, own3, far, side, side_b, block0, block1, block2a, block2b, block3 = refs
    rows = own0.shape[1]
    copies = []
    for i, (mine, theirs) in enumerate(
        (
            (own0.at[0], side.at[0]),
            (own1.at[0], side.at[1]),
            (far.at[2], side_b.at[4]),
            (own3.at[0], side.at[2]),
        )
    ):
        start = 2 * rows * i
        copies.append((mine, full.at[pl.ds(start + low * rows, rows), :]))
        copies.append((theirs, full.at[pl.ds(start + (1 - low) * rows, rows), :]))
    for at, size, block in (
        (8, 2, block0),
        (10, 2, block1),
        (12, 1, block2a),
        (13, 1, block2b),
        (14, 2, block3),
    ):
        copies.append((block.at[0], full.at[pl.ds(at * rows, size * rows), :]))
    return copies


def chunk(i, size=WIDE):
    return pl.ds(pl.multiple_of(i * size, size), size)


def row_pieces(refs, first, full):
    copies = []
    for core, (home, seen) in enumerate((refs[:2], refs[2:])):
        for z in range(4):
            at = (core * 8 + z) * MOST
            copies.append((home.at[z, pl.ds(first, MOST)], full.at[pl.ds(at, MOST)]))
            copies.append((seen.at[z], full.at[pl.ds(at + 4 * MOST, MOST)]))
    return copies


def forward_kernel(place, *refs):
    row_refs, pieces, (hid_ref, fa_ref, fb_ref, rows_ref, full, sems, row_sems) = (
        refs[:4],
        refs[4:14],
        refs[14:],
    )
    started = fetch(row_pieces(row_refs, 0, rows_ref), row_sems)
    started += fetch(gate_up_pieces(place[2], pieces, full), sems)
    for copy in started:
        copy.wait()

    def step(i, unused):
        gate = dot(rows_ref[...], full[0, :, chunk(i)], ((1,), (0,)))
        up = dot(rows_ref[...], full[1, :, chunk(i)], ((1,), (0,)))
        sig = 1.0 / (1.0 + jnp.exp(-gate))
        silu = gate * sig
        hid_ref[:, chunk(i)] = (silu * up).astype(BF16)
        fa_ref[:, chunk(i)] = up * sig * (1.0 + gate * (1.0 - sig))
        fb_ref[:, chunk(i)] = silu
        return unused

    lax.fori_loop(0, hid_ref.shape[1] // WIDE, step, 0)


def term_of(at, rows_ref, right_ref):
    return dot(rows_ref[:, at], right_ref[...], ((0,), (0,))).astype(BF16)


def down_term_kernel(place, hid_ref, *refs):
    row_refs, (keep, give, mir0, mir1, mir2, mir3) = refs[:4], refs[4:10]
    rows_ref, terms, row_sems, sems = refs[10:]
    for copy in fetch(row_pieces(row_refs, MOST, rows_ref), row_sems):
        copy.wait()
    low = place[2]
    rows = keep.shape[1]
    half = terms.shape[0] // 2
    owns, mirs = [], []
    for i in range(4):
        start = 2 * rows * i
        owns.append((terms.at[pl.ds(start + low * rows, rows), :], keep.at[i]))
        owns.append((terms.at[pl.ds(start + (1 - low) * rows, rows), :], give.at[i]))
    for i, mir in enumerate((mir0, mir1, mir2, mir3)):
        mirs.append((terms.at[pl.ds(half + 2 * i * rows, 2 * rows), :], mir.at[0]))
    terms[:half, :] = term_of(slice(0, half), rows_ref, hid_ref)
    started = fetch(owns, sems)
    terms[half:, :] = term_of(slice(half, 2 * half), rows_ref, hid_ref)
    started += fetch(mirs, row_sems)
    for copy in started:
        copy.wait()


def gradient_kernel(place, fa_ref, fb_ref, *refs):
    grad_refs, tok_refs, pieces, refs = refs[:4], refs[4:8], refs[8:19], refs[19:]
    both_ref, blk0, blk1, blk2, blk3, keep, give_a, give_b = refs[:8]
    g_rows, x_rows, full, terms, in_sems, out_sems, g_sems, x_sems = refs[8:]
    low = place[2]
    rows = give_b.shape[2]
    started = fetch(row_pieces(grad_refs, MOST, g_rows), g_sems)
    started += fetch(down_pieces(low, pieces, full), in_sems)
    later = fetch(row_pieces(tok_refs, 0, x_rows), x_sems)
    for copy in started:
        copy.wait()

    def step(i, unused):
        hidden_grad = dot(g_rows[...], full[:, chunk(i)], ((1,), (0,)))
        both_ref[0, :, chunk(i)] = (hidden_grad * fa_ref[:, chunk(i)]).astype(BF16)
        both_ref[1, :, chunk(i)] = (hidden_grad * fb_ref[:, chunk(i)]).astype(BF16)
        return unused

    lax.fori_loop(0, both_ref.shape[2] // WIDE, step, 0)
    for copy in later:
        copy.wait()

    half = terms.shape[1] // 2
    blocks, mirs = [], []
    for i, blk in enumerate((blk0, blk1, blk2, blk3)):
        blocks.append((terms.at[:, pl.ds(2 * rows * i, 2 * rows), :], blk))
    for i, give in enumerate((give_b.at[0], give_a.at[1], give_a.at[0], give_b.at[1])):
        start = (8 + 2 * i) * rows
        mirs.append((terms.at[:, pl.ds(start + (1 - low) * rows, rows), :], keep.at[i]))
        mirs.append((terms.at[:, pl.ds(start + low * rows, rows), :], give))
    started = []
    for copies, first, sems in ((blocks, 0, in_sems), (mirs, half, out_sems)):
        at = slice(first, first + half)

        def put(i, unused, at=at):
            terms[i, at, :] = dot(x_rows[:, at], both_ref[i], ((0,), (0,))).astype(BF16)
            return unused

        lax.fori_loop(0, 2, put, 0)
        started += fetch(copies, sems)
    for copy in started:
        copy.wait()


def output_kernel(place, hid_ref, both_ref, *refs):
    up_pieces, dn_pieces, refs = refs[:10], refs[10:21], refs[21:]
    out_mine, grad_mine, theirs, full, down, sems, down_sems = refs
    low = place[2]
    first = fetch(down_pieces(low, dn_pieces, down), down_sems)
    second = fetch(gate_up_pieces(low, up_pieces, full), sems)
    count = out_mine.shape[0]
    for copy in first:
        copy.wait()

    half = down.shape[0] // 2

    def out_step(i, unused):
        at = chunk(i, half)
        out_mine[:, at] = dot(hid_ref[:count, :], down[at, :], ((1,), (1,)))
        theirs[:count, at] = dot(hid_ref[count:, :], down[at, :], ((1,), (1,))).astype(BF16)
        return unused

    lax.fori_loop(0, 2, out_step, 0)
    for copy in second:
        copy.wait()

    def grad_step(i, unused):
        at = chunk(i, half)
        gate, up = full[0, at, :], full[1, at, :]
        for mine, to in ((slice(0, count), grad_mine), (slice(count, 2 * count), theirs)):
            total = dot(both_ref[0, mine, :], gate, ((1,), (1,))) + dot(
                both_ref[1, mine, :], up, ((1,), (1,))
            )
            to[mine if to is theirs else slice(None), at] = total.astype(to.dtype)
        return unused

    lax.fori_loop(0, 2, grad_step, 0)


def run(kernel, name, place, local, remote, outs, far_outs, scratch, flops):
    vmem, anywhere = pl.BlockSpec(memory_space=pltpu.VMEM), pl.BlockSpec(memory_space=pl.ANY)
    shapes = [jax.ShapeDtypeStruct(*o) for o in tuple(outs) + tuple(far_outs)]
    size = sum(a.size * a.dtype.itemsize for a in (*local, *remote))
    size += sum(a.size * a.dtype.itemsize for a in shapes)
    return pl.pallas_call(
        kernel,
        out_shape=shapes,
        in_specs=[pl.BlockSpec(memory_space=pltpu.SMEM)]
        + [vmem] * len(local)
        + [anywhere] * len(remote),
        out_specs=[vmem] * len(outs) + [anywhere] * len(far_outs),
        scratch_shapes=scratch,
        compiler_params=pltpu.CompilerParams(vmem_limit_bytes=44 << 20),
        cost_estimate=pl.CostEstimate(
            flops=flops, bytes_accessed=size, transcendentals=0
        ),
        name=name,
    )(place, *local, *remote)


def on_device(tokens, expert_ids, gate_vals, w_gate, w_up, w_down, cotangent):
    core = lax.axis_index("expert") % 2
    y, x = lax.axis_index("fsdp") // 4, lax.axis_index("fsdp") % 4
    side, low = x // 2, x % 2
    rows, width = w_gate.shape[1:]
    depth = tokens.shape[1]
    part = half_width(width)
    quarter = 4 * MOST
    count = 4 * quarter
    work = count * depth * part * 2
    dma, row_dma = pltpu.SemaphoreType.DMA((13,)), pltpu.SemaphoreType.DMA((16,))
    row_scratch = pltpu.VMEM((count, depth), BF16)
    place = jnp.stack([y, side, low, core]).astype(jnp.int32)
    ids, gates = expert_ids.T, gate_vals.T
    r = Rounds()
    send = r.send

    def join(*arrays):
        return jnp.concatenate(arrays, axis=0)

    slices = ((3, rows, part), BF16)
    keep, give = run(
        split_kernel,
        "split",
        place,
        (),
        (w_gate, w_up, w_down),
        [slices] * 2,
        [],
        [pltpu.VMEM((3, rows, width), BF16), pltpu.SemaphoreType.DMA((3,))],
        1,
    )
    got = send("core", give)
    own_gu, own_dn, away_gu, away_dn = run(
        choose_kernel,
        "choose",
        place,
        (keep, got),
        (),
        [((2, rows, part), BF16), ((1, rows, part), BF16)] * 2,
        [],
        [],
        1,
    )
    r.next()
    side_gu = send("side", own_gu)
    mir0 = send("mirror", away_gu)
    own3 = send("up", own_dn)
    own1 = send("down", own_dn)
    r.next()
    block0 = in_pair(low == 0, own_gu, side_gu, 1)
    mir3 = send("up", mir0)
    mir1 = send("down", mir0)
    dn_mir = send("mirror", away_dn)
    both, oth, goth = dispatch(r.late(place), ids, gates, tokens, cotangent)
    home = r.exchange(r.late(both).reshape(4, 2 * MOST, depth), 2)
    r.next()
    block3 = send("up", block0)
    far = send("down", join(mir1, own1))
    side_a = send("side", join(mir0, mir1, dn_mir))
    tok_mir = send("mirror", oth)
    r.next()
    block_dn = in_pair(low == 1, dn_mir, side_a[4:], 1)
    block2 = send("up", block3)
    block1 = send("down", block0)
    side_b = send("side", join(mir3, far))
    grad_mir = send("mirror", goth)
    home_got = r.hold(lax.ppermute(r.late(home), AXES, TO_CORE))
    seen_tok = r.exchange(tok_mir.reshape(4, MOST, depth), 2)
    r.next()
    dn3 = send("up", block_dn)
    dn1 = send("down", block_dn)
    own_side = send("side", join(own_dn, own1, own3))
    tok_got = r.hold(lax.ppermute(after(seen_tok, side_b), AXES, TO_CORE))
    token_rows = (home, seen_tok, home_got, tok_got)
    gu_pieces = (block0, block1, block2, block3, mir0, mir1, mir3, far, side_a, side_b)
    hidden, fa, fb = run(
        forward_kernel,
        "forward",
        r.late(place),
        (),
        token_rows + gu_pieces,
        [((count, part), BF16), ((count, part), F32), ((count, part), F32)],
        [],
        [row_scratch, pltpu.VMEM((2, depth, part), BF16), dma, row_dma],
        2 * work,
    )
    r.hold(hidden)
    seen_grad = r.exchange(r.late(grad_mir).reshape(4, MOST, depth))
    r.next()
    dn2a = send("up", r.pin(dn3)[:, :rows])
    dn2b = send("down", r.pin(dn1)[:, rows:])
    grad_got = r.hold(lax.ppermute(r.pin(seen_grad), AXES, TO_CORE))
    grad_rows = (home, seen_grad, home_got, grad_got)
    own_keep, own_give, mir_t0, mir_t1, mir_t2, mir_t3 = run(
        down_term_kernel,
        "down_term",
        place,
        (r.pin(hidden),),
        grad_rows,
        [],
        [((4, rows, part), BF16)] * 2 + [((1, 2 * rows, part), BF16)] * 4,
        [row_scratch, pltpu.VMEM((depth, part), BF16), row_dma, dma],
        work,
    )
    r.hold(own_give)
    r.next()
    dn_pieces = (own_dn, own1, own3, far, own_side, side_b, block_dn, dn1, dn2a, dn2b, dn3)
    dn_far = send("down", mir_t2)
    dn_back = send("up", mir_t1)
    own_got = send("side", own_give)
    hidden_grads, blk_t0, blk_t1, blk_t2, blk_t3, mir_keep, give_a, give_b = run(
        gradient_kernel,
        "gradient",
        place,
        (r.pin(fa), fb),
        grad_rows + token_rows + dn_pieces,
        [((2, count, part), BF16)],
        [((2, 2 * rows, part), BF16)] * 4
        + [((4, 2, rows, part), BF16)]
        + [((2, 2, rows, part), BF16)] * 2,
        [row_scratch, row_scratch]
        + [pltpu.VMEM((depth, part), BF16), pltpu.VMEM((2, depth, part), BF16)]
        + [dma, dma, row_dma, row_dma],
        3 * work,
    )
    r.hold(give_a)

    r.next()
    own_sum = add(own_keep, own_got)
    blk_far = send("up", blk_t2)
    blk_back = send("down", blk_t3)
    got_a = send("side", give_a)
    own_far = send("down", own_sum[2:3])
    out_mine, grad_mine, theirs = run(
        output_kernel,
        "outputs",
        place,
        (r.pin(hidden), hidden_grads),
        gu_pieces + dn_pieces,
        [((count // 2, depth), F32)] * 2 + [((count, depth), BF16)],
        [],
        [pltpu.VMEM((2, depth, part), BF16), pltpu.VMEM((depth, part), BF16), dma, dma],
        3 * work,
    )
    r.hold(theirs)
    r.next()
    blk_near = send("up", add(blk_far, blk_t1))
    mir_far = send("down", add(mir_keep[2], got_a[0]))
    got_b = send("side", give_b)
    dn_down = send(
        "down", jnp.concatenate([add(dn_far, mir_t3), add(own_far, own_sum[3:])], axis=1)
    )
    got = send("core", theirs)
    out = r.hold(add(r.late(out_mine), got[: 2 * quarter]))
    out_home = r.exchange(out[quarter:].reshape(4, MOST, depth))
    grd = r.hold(add(r.late(grad_mine), got[2 * quarter :]))
    grad_home = r.exchange(grd[quarter:].reshape(4, MOST, depth), 2)
    r.next()
    dn_down, blk_near, blk_back = r.pin(dn_down), r.pin(blk_near), r.pin(blk_back)
    dn_near, own_near = dn_down[:, : 2 * rows], dn_down[:, 2 * rows :]
    mir_back = send("up", jnp.concatenate([add(mir_keep[1], got_a[1]), own_sum[1:2]], axis=0))
    mir_near = send("down", add(r.pin(mir_far), mir_keep[3], r.pin(got_b)[1]))
    blk = add(blk_t0, blk_back, blk_near)
    mir_dn = add(mir_t0, dn_back, dn_near)
    low_half, high_half = join(blk[:, :rows], mir_dn[:, rows:]), join(blk[:, rows:], mir_dn[:, :rows])
    stay = jnp.where(low == 0, low_half, high_half)
    leave_got = send("side", jnp.where(low == 0, high_half, low_half))
    out_oth = send("mirror", out_home.reshape(quarter, depth))
    out_own = r.exchange(r.late(out[:quarter]).reshape(4, MOST, depth), 2)
    r.next()
    here = core == side
    mir_back = r.pin(mir_back)
    mine = add(stay, r.pin(leave_got))
    gu_mir = add(mir_keep[0], got_b[0], mir_back[:2], r.pin(mir_near))
    away = send("mirror", join(gu_mir, mine[2:]))
    grad_oth = send("mirror", grad_home.reshape(quarter, depth))
    grad_own = r.exchange(r.late(grd[:quarter]).reshape(4, MOST, depth))
    out_own, grad_own = out_own.reshape(quarter, depth), grad_own.reshape(quarter, depth)
    own = join(mine[:2], add(own_sum[:1], mir_back[2:], own_near))
    other = lax.ppermute(jnp.where(here, away, own), AXES, TO_CORE)
    kept = jnp.where(here, own, away)
    grad_gate, grad_up, grad_down = (
        whole_width(kept[i : i + 1], other[i : i + 1], width, core) for i in range(3)
    )

    output, grad_tokens, grad_gates = combine(
        place, ids, gates, cotangent, out_own, out_oth, grad_own, grad_oth
    )
    return (output, grad_tokens, grad_gates.T, grad_gate, grad_up, grad_down)


def solution(mesh):
    rows, weight = P(AXES, None), P("expert", "fsdp", None)
    return jax.shard_map(
        on_device,
        mesh=mesh,
        in_specs=(rows, rows, rows, weight, weight, weight, rows),
        out_specs=(rows, rows, rows, weight, weight, weight),
        check_vma=False,
    )
```

profile of v0, /device:TPU:0, one launch (start us, length us, event | category | flops | bytes accessed | tf_op | source)
XLA Modules:
  0.0 278.1 jit_solution(545072789304290658)
XLA Ops:
  15.0 3.9 %collective-permute-done.4.refs_9_.refs_11_ = bf16[1,128,768]{2,1,0:T(8,128)(2,1)S(1)} collective-permute-done((bf16[1,128,768]{2,1,0:T(8,128)(2,1)S(1)}, bf16[1,128,768]{2,1,0:T(8,128)(2,1)S(1)}, u32[]{:S(2)}, u32[]{:S(2)}) %collective-permute-start.4) | collective-permute-done | bytes 196640 | tf_op jit(solution)/shard_map/ppermute | solution.py:60
  18.9 3.4 %collective-permute-done.3.refs_10_.refs_12_ = bf16[1,128,768]{2,1,0:T(8,128)(2,1)S(1)} collective-permute-done((bf16[1,128,768]{2,1,0:T(8,128)(2,1)S(1)}, bf16[1,128,768]{2,1,0:T(8,128)(2,1)S(1)}, u32[]{:S(2)}, u32[]{:S(2)}) %collective-permute-start.3) | collective-permute-done | bytes 196640 | tf_op jit(solution)/shard_map/ppermute | solution.py:60
  31.5 5.3 %all-to-all-start = ((bf16[4,96,2048]{2,1,0:T(8,128)(2,1)}), bf16[4,96,2048]{2,1,0:T(8,128)(2,1)S(1)}, u32[]{:S(2)}, u32[]{:S(2)}) async-start(bf16[4,96,2048]{2,1,0:T(8,128)(2,1)} %bitcast.6), calls=%async_computation | async-start | bytes 3145728 | tf_op jit(solution)/shard_map/all_to_all | solution.py:63
  44.9 10.3 %collective-permute-done.10.refs_11_.refs_7_.refs_13_ = bf16[3,128,768]{2,1,0:T(8,128)(2,1)S(1)} collective-permute-done((bf16[3,128,768]{2,1,0:T(8,128)(2,1)S(1)}, bf16[3,128,768]{2,1,0:T(8,128)(2,1)S(1)}, u32[]{:S(2)}, u32[]{:S(2)}) %collective-permute-start.10) | collective-permute-done | bytes 589856 | tf_op jit(solution)/shard_map/ppermute | solution.py:60
  61.4 4.5 %all-to-all-start.1 = ((bf16[4,48,2048]{2,1,0:T(8,128)(2,1)}), bf16[4,48,2048]{2,1,0:T(8,128)(2,1)S(1)}, u32[]{:S(2)}, u32[]{:S(2)}) async-start(bf16[4,48,2048]{2,1,0:T(8,128)(2,1)} %bitcast.7), calls=%async_computation.1 | async-start | bytes 1572864 | tf_op jit(solution)/shard_map/all_to_all | solution.py:63
  70.3 8.6 %all-to-all-done.1.refs_1_.refs_5_ = bf16[4,48,2048]{2,1,0:T(8,128)(2,1)S(1)} async-done(((bf16[4,48,2048]{2,1,0:T(8,128)(2,1)}), bf16[4,48,2048]{2,1,0:T(8,128)(2,1)S(1)}, u32[]{:S(2)}, u32[]{:S(2)}) %all-to-all-start.1) | async-done | bytes 786464 | tf_op jit(solution)/shard_map/all_to_all | solution.py:63
  78.9 3.5 %collective-permute-done.14.refs_13_.refs_9_.refs_15_ = bf16[5,128,768]{2,1,0:T(8,128)(2,1)} collective-permute-done((bf16[5,128,768]{2,1,0:T(8,128)(2,1)}, bf16[5,128,768]{2,1,0:T(8,128)(2,1)}, u32[]{:S(2)}, u32[]{:S(2)}) %collective-permute-start.14) | collective-permute-done | bytes 983072 | tf_op jit(solution)/shard_map/ppermute | solution.py:60
  89.9 4.5 %all-to-all-start.2 = ((bf16[4,48,2048]{2,1,0:T(8,128)(2,1)}), bf16[4,48,2048]{2,1,0:T(8,128)(2,1)}, u32[]{:S(2)}, u32[]{:S(2)}) async-start(bf16[4,48,2048]{2,1,0:T(8,128)(2,1)} %bitcast.8), calls=%async_computation.2 | async-start | bytes 1572864 | tf_op jit(solution)/shard_map/all_to_all | solution.py:63
  100.3 12.6 %forward.1 = (bf16[768,768]{1,0:T(8,128)(2,1)S(1)}, f32[768,768]{1,0:T(8,128)}, f32[768,768]{1,0:T(8,128)}) custom-call(s32[4]{0:T(128)S(1)} %pad_add_fusion.place, bf16[4,96,2048]{2,1,0:T(8,128)(2,1)} %copy-done, bf16[4,48,2048]{2,1,0:T(8,128)(2,1)S(1)} %all-to-all-done.1.refs_1_.refs_5_, bf16[4,96,2048]{2,1,0:T(8,128)(2,1)} %collective-permute-done.16.refs_2_.refs_6_, ...), custom_call_target="tpu_custom_call" | custom-call | flops 4831838208 | bytes 17498112 | tf_op jit(solution)/shard_map/forward/pallas_call | solution.py:478
  116.0 3.2 %collective-permute-start.23 = (bf16[1,128,768]{2,1,0:T(8,128)(2,1)S(1)}, bf16[1,128,768]{2,1,0:T(8,128)(2,1)S(1)}, u32[]{:S(2)}, u32[]{:S(2)}) collective-permute-start(bf16[1,128,768]{2,1,0:T(8,128)(2,1)S(1)} %slice.122), channel_id=1, source_target_pairs={{0,12},{1,13},{2,14},{3,15},{4,0},{5,1},{6,2},{7,3},{8,4},{9,5},{1... | collective-permute-start | bytes 589832 | tf_op jit(solution)/shard_map/ppermute | solution.py:60
  120.5 10.0 %down_term.1 = (bf16[4,128,768]{2,1,0:T(8,128)(2,1)S(1)}, bf16[4,128,768]{2,1,0:T(8,128)(2,1)S(1)}, bf16[1,256,768]{2,1,0:T(8,128)(2,1)S(1)}, bf16[1,256,768]{2,...) custom-call(s32[4]{0:T(128)S(1)} %pad_add_fusion.place, ...), custom_call_target="tpu_custom_call" | custom-call | flops 2415919104 | bytes 9043968 | tf_op jit(solution)/shard_map/down_term/pallas_call | solution.py:478
  131.8 3.2 %collective-permute-start.24 = (bf16[1,256,768]{2,1,0:T(8,128)(2,1)S(1)}, bf16[1,256,768]{2,1,0:T(8,128)(2,1)S(1)}, u32[]{:S(2)}, u32[]{:S(2)}) collective-permute-start(bf16[1,256,768]{2,1,0:T(8,128)(2,1)S(1)} %get-tuple-element.136), channel_id=1, source_target_pairs={{0,12},{1,13},{2,14},{3,15},{4,0},{5,1},{6,2},{7,3},{8,4},{9,5},{1... | collective-permute-start | bytes 1179656 | tf_op jit(solution)/shard_map/ppermute | solution.py:60
  135.1 19.8 %gradient.1 = (bf16[2,768,768]{2,1,0:T(8,128)(2,1)}, bf16[2,256,768]{2,1,0:T(8,128)(2,1)S(1)}, bf16[2,256,768]{2,1,0:T(8,128)(2,1)S(1)}, bf16[2,256,768]{2,1,0:T...) custom-call(s32[4]{0:T(128)S(1)} %pad_add_fusion.place, ...), custom_call_target="tpu_custom_call" | custom-call | flops 7247757312 | bytes 27131904 | tf_op jit(solution)/shard_map/gradient/pallas_call | solution.py:478
  155.0 3.2 %collective-permute-start.28 = (bf16[2,256,768]{2,1,0:T(8,128)(2,1)S(1)}, bf16[2,256,768]{2,1,0:T(8,128)(2,1)S(1)}, u32[]{:S(2)}, u32[]{:S(2)}) collective-permute-start(bf16[2,256,768]{2,1,0:T(8,128)(2,1)S(1)} %get-tuple-element.151), channel_id=1, source_target_pairs={{0,12},{1,13},{2,14},{3,15},{4,0},{5,1},{6,2},{7,3},{8,4},{9,5},{1... | collective-permute-start | bytes 2359304 | tf_op jit(solution)/shard_map/ppermute | solution.py:60
  160.7 15.0 %outputs.1 = (f32[384,2048]{1,0:T(8,128)}, f32[384,2048]{1,0:T(8,128)}, bf16[768,2048]{1,0:T(8,128)(2,1)}) custom-call(s32[4]{0:T(128)S(1)} %pad_add_fusion.place, bf16[768,768]{1,0:T(8,128)(2,1)} %copy-done.35, bf16[2,768,768]{2,1,0:T(8,128)(2,1)} %get-tuple-element.145.both_ref, bf16[2,256,768]{2,1,0:T(8,128)(2,1)S(1)} %maximum_select_fusion.refs_4_.refs_0_, ...), custom_call_target="tpu_custom_call" | custom-call | flops 7247757312 | bytes 24182784 | tf_op jit(solution)/shard_map/outputs/pallas_call | solution.py:478
  182.1 3.7 %collective-permute-start.35 = (bf16[1,384,768]{2,1,0:T(8,128)(2,1)}, bf16[1,384,768]{2,1,0:T(8,128)(2,1)}, u32[]{:S(2)}, u32[]{:S(2)}) collective-permute-start(bf16[1,384,768]{2,1,0:T(8,128)(2,1)} %pad_maximum_fusion.4), channel_id=1, source_target_pairs={{0,12},{1,13},{2,14},{3,15},{4,0},{5,1},{6,2},{7,3},{8,4},{9,5},{1... | collective-permute-start | bytes 1769480 | tf_op jit(solution)/shard_map/ppermute | solution.py:60
  193.2 4.9 %all-to-all-start.3 = ((bf16[4,48,2048]{2,1,0:T(8,128)(2,1)}), bf16[4,48,2048]{2,1,0:T(8,128)(2,1)}, u32[]{:S(2)}, u32[]{:S(2)}) async-start(bf16[4,48,2048]{2,1,0:T(8,128)(2,1)} %bitcast.41), calls=%async_computation.3 | async-start | bytes 1572864 | tf_op jit(solution)/shard_map/all_to_all | solution.py:63
  200.2 9.7 %all-to-all-done.3 = bf16[4,48,2048]{2,1,0:T(8,128)(2,1)} async-done(((bf16[4,48,2048]{2,1,0:T(8,128)(2,1)}), bf16[4,48,2048]{2,1,0:T(8,128)(2,1)}, u32[]{:S(2)}, u32[]{:S(2)}) %all-to-all-start.3) | async-done | bytes 786464 | tf_op jit(solution)/shard_map/all_to_all | solution.py:63
  210.0 4.2 %all-to-all-start.5 = ((bf16[4,48,2048]{2,1,0:T(8,128)(2,1)}), bf16[4,48,2048]{2,1,0:T(8,128)(2,1)}, u32[]{:S(2)}, u32[]{:S(2)}) async-start(bf16[4,48,2048]{2,1,0:T(8,128)(2,1)} %bitcast.40), calls=%async_computation.5 | async-start | bytes 1572864 | tf_op jit(solution)/shard_map/all_to_all | solution.py:63
  225.3 4.7 %all-to-all-start.4 = ((bf16[4,48,2048]{2,1,0:T(8,128)(2,1)}), bf16[4,48,2048]{2,1,0:T(8,128)(2,1)S(1)}, u32[]{:S(2)}, u32[]{:S(2)}) async-start(bf16[4,48,2048]{2,1,0:T(8,128)(2,1)} %bitcast.15), calls=%async_computation.4 | async-start | bytes 1572864 | tf_op jit(solution)/shard_map/all_to_all | solution.py:63
  244.7 4.5 %all-to-all-start.6 = ((bf16[4,48,2048]{2,1,0:T(8,128)(2,1)}), bf16[4,48,2048]{2,1,0:T(8,128)(2,1)S(1)}, u32[]{:S(2)}, u32[]{:S(2)}) async-start(bf16[4,48,2048]{2,1,0:T(8,128)(2,1)} %bitcast.20), calls=%async_computation.6 | async-start | bytes 1572864 | tf_op jit(solution)/shard_map/all_to_all | solution.py:63
  249.1 7.5 %collective-permute-done.41 = bf16[3,128,768]{2,1,0:T(8,128)(2,1)} collective-permute-done((bf16[3,128,768]{2,1,0:T(8,128)(2,1)}, bf16[3,128,768]{2,1,0:T(8,128)(2,1)}, u32[]{:S(2)}, u32[]{:S(2)}) %collective-permute-start.41) | collective-permute-done | bytes 589856 | tf_op jit(solution)/shard_map/ppermute | solution.py:60
  259.0 10.7 %collective-permute-done.40.goth_ref = bf16[192,2048]{1,0:T(8,128)(2,1)} collective-permute-done((bf16[192,2048]{1,0:T(8,128)(2,1)}, bf16[192,2048]{1,0:T(8,128)(2,1)}, u32[]{:S(2)}, u32[]{:S(2)}) %collective-permute-start.40) | collective-permute-done | bytes 786464 | tf_op jit(solution)/shard_map/ppermute | solution.py:60
  269.7 4.4 %combine.1 = (bf16[256,2048]{1,0:T(8,128)(2,1)}, bf16[256,2048]{1,0:T(8,128)(2,1)}, f32[6,256]{1,0:T(8,128)}) custom-call(s32[4]{0:T(128)S(1)} %pad_add_fusion.place, s32[6,256]{1,0:T(8,128)S(1)} %bitcast.37, bf16[6,256]{1,0:T(8,128)(2,1)S(1)} %bitcast.39, bf16[256,2048]{1,0:T(8,128)(2,1)S(1)} %copy-done.27, bf16[192,2048]{1,0:T(8,128)(2,1)S(1)} %bitcast.34, ...), custom_call_target="tpu_custom_call" | custom-call | flops 2000000000 | bytes 8000000 | tf_op jit(solution)/shard_map/combine/pallas_call | solution.py:209
  (223 shorter events, 111.5 us)
Async XLA Ops:
  31.5 26.9 %all-to-all-start = ((bf16[4,96,2048]{2,1,0:T(8,128)(2,1)}), bf16[4,96,2048]{2,1,0:T(8,128)(2,1)S(1)}, u32[]{:S(2)}, u32[]{:S(2)}) async-start(bf16[4,96,2048]{2,1,0:T(8,128)(2,1)} %bitcast.6), calls=%async_computation | async-start | bytes 3145728 | tf_op jit(solution)/shard_map/all_to_all | solution.py:63
  39.0 22.1 %collective-permute-start.8 = (bf16[5,128,768]{2,1,0:T(8,128)(2,1)}, bf16[5,128,768]{2,1,0:T(8,128)(2,1)}, u32[]{:S(2)}, u32[]{:S(2)}) collective-permute-start(bf16[5,128,768]{2,1,0:T(8,128)(2,1)} %pad_maximum_fusion), channel_id=1, source_target_pairs={{0,1},{1,0},{2,3},{3,2},{4,5},{5,4},{6,7},{7,6},{8,9},{9,8},{10,11... | collective-permute-start | bytes 2949128 | tf_op jit(solution)/shard_map/ppermute | solution.py:60
  39.4 19.0 %collective-permute-start.9 = (bf16[2,256,768]{2,1,0:T(8,128)(2,1)S(1)}, bf16[2,256,768]{2,1,0:T(8,128)(2,1)}, u32[]{:S(2)}, u32[]{:S(2)}) collective-permute-start(bf16[2,256,768]{2,1,0:T(8,128)(2,1)S(1)} %maximum_select_fusion.refs_4_.refs_0_), channel_id=1, source_target_pairs={{0,4},{1,5},{2,6},{3,7},{4,8},{5,9},{6,10},{7,11},{8,12},{9,13},{1... | collective-permute-start | bytes 2359304 | tf_op jit(solution)/shard_map/ppermute | solution.py:60
  61.2 21.2 %collective-permute-start.14 = (bf16[5,128,768]{2,1,0:T(8,128)(2,1)}, bf16[5,128,768]{2,1,0:T(8,128)(2,1)}, u32[]{:S(2)}, u32[]{:S(2)}) collective-permute-start(bf16[5,128,768]{2,1,0:T(8,128)(2,1)} %pad_maximum_fusion.1), channel_id=1, source_target_pairs={{0,1},{1,0},{2,3},{3,2},{4,5},{5,4},{6,7},{7,6},{8,9},{9,8},{10,11... | collective-permute-start | bytes 2949128 | tf_op jit(solution)/shard_map/ppermute | solution.py:60
  61.4 28.4 %collective-permute-start.16 = (bf16[4,96,2048]{2,1,0:T(8,128)(2,1)S(1)}, bf16[4,96,2048]{2,1,0:T(8,128)(2,1)}, u32[]{:S(2)}, u32[]{:S(2)}) collective-permute-start(bf16[4,96,2048]{2,1,0:T(8,128)(2,1)S(1)} %all-to-all-done.refs_0_.refs_4_), channel_id=1, source_target_pairs={{0,16},{1,17},{2,18},{3,19},{4,20},{5,21},{6,22},{7,23},{8,24},{9,... | collective-permute-start | bytes 4718600 | tf_op jit(solution)/shard_map/ppermute | solution.py:561
  66.0 21.2 %collective-permute-start.12 = (bf16[2,256,768]{2,1,0:T(8,128)(2,1)}, bf16[2,256,768]{2,1,0:T(8,128)(2,1)}, u32[]{:S(2)}, u32[]{:S(2)}) collective-permute-start(bf16[2,256,768]{2,1,0:T(8,128)(2,1)} %collective-permute-done.9.refs_7_.refs_3_), channel_id=1, source_target_pairs={{0,4},{1,5},{2,6},{3,7},{4,8},{5,9},{6,10},{7,11},{8,12},{9,13},{1... | collective-permute-start | bytes 2359304 | tf_op jit(solution)/shard_map/ppermute | solution.py:60
  66.3 20.9 %collective-permute-start.13 = (bf16[2,256,768]{2,1,0:T(8,128)(2,1)S(1)}, bf16[2,256,768]{2,1,0:T(8,128)(2,1)}, u32[]{:S(2)}, u32[]{:S(2)}) collective-permute-start(bf16[2,256,768]{2,1,0:T(8,128)(2,1)S(1)} %maximum_select_fusion.refs_4_.refs_0_), channel_id=1, source_target_pairs={{0,12},{1,13},{2,14},{3,15},{4,0},{5,1},{6,2},{7,3},{8,4},{9,5},{1... | collective-permute-start | bytes 2359304 | tf_op jit(solution)/shard_map/ppermute | solution.py:60
  69.2 20.7 %collective-permute-start.15 = (bf16[192,2048]{1,0:T(8,128)(2,1)}, bf16[192,2048]{1,0:T(8,128)(2,1)}, u32[]{:S(2)}, u32[]{:S(2)}) collective-permute-start(bf16[192,2048]{1,0:T(8,128)(2,1)} %copy-done.30), channel_id=1, source_target_pairs={{0,3},{1,2},{2,1},{3,0},{4,7},{5,6},{6,5},{7,4},{8,11},{9,10},{10,... | collective-permute-start | bytes 2359304 | tf_op jit(solution)/shard_map/ppermute | solution.py:60
  89.9 24.0 %all-to-all-start.2 = ((bf16[4,48,2048]{2,1,0:T(8,128)(2,1)}), bf16[4,48,2048]{2,1,0:T(8,128)(2,1)}, u32[]{:S(2)}, u32[]{:S(2)}) async-start(bf16[4,48,2048]{2,1,0:T(8,128)(2,1)} %bitcast.8), calls=%async_computation.2 | async-start | bytes 1572864 | tf_op jit(solution)/shard_map/all_to_all | solution.py:63
  94.4 19.5 %collective-permute-start.20 = (bf16[3,128,768]{2,1,0:T(8,128)(2,1)}, bf16[3,128,768]{2,1,0:T(8,128)(2,1)}, u32[]{:S(2)}, u32[]{:S(2)}) collective-permute-start(bf16[3,128,768]{2,1,0:T(8,128)(2,1)} %get-tuple-element.123), channel_id=1, source_target_pairs={{0,1},{1,0},{2,3},{3,2},{4,5},{5,4},{6,7},{7,6},{8,9},{9,8},{10,11... | collective-permute-start | bytes 1769480 | tf_op jit(solution)/shard_map/ppermute | solution.py:60
  95.2 18.7 %collective-permute-start.19 = (bf16[1,256,768]{2,1,0:T(8,128)(2,1)}, bf16[1,256,768]{2,1,0:T(8,128)(2,1)}, u32[]{:S(2)}, u32[]{:S(2)}) collective-permute-start(bf16[1,256,768]{2,1,0:T(8,128)(2,1)} %maximum_select_fusion.1.refs_14_.refs_16_), channel_id=1, source_target_pairs={{0,12},{1,13},{2,14},{3,15},{4,0},{5,1},{6,2},{7,3},{8,4},{9,5},{1... | collective-permute-start | bytes 1179656 | tf_op jit(solution)/shard_map/ppermute | solution.py:60
  130.5 24.3 %collective-permute-start.26 = (bf16[4,128,768]{2,1,0:T(8,128)(2,1)S(1)}, bf16[4,128,768]{2,1,0:T(8,128)(2,1)S(1)}, u32[]{:S(2)}, u32[]{:S(2)}) collective-permute-start(bf16[4,128,768]{2,1,0:T(8,128)(2,1)S(1)} %get-tuple-element.139), channel_id=1, source_target_pairs={{0,1},{1,0},{2,3},{3,2},{4,5},{5,4},{6,7},{7,6},{8,9},{9,8},{10,11... | collective-permute-start | bytes 2359304 | tf_op jit(solution)/shard_map/ppermute | solution.py:60
  131.8 23.0 %collective-permute-start.25 = (bf16[1,256,768]{2,1,0:T(8,128)(2,1)S(1)}, bf16[1,256,768]{2,1,0:T(8,128)(2,1)S(1)}, u32[]{:S(2)}, u32[]{:S(2)}) collective-permute-start(bf16[1,256,768]{2,1,0:T(8,128)(2,1)S(1)} %get-tuple-element.138), channel_id=1, source_target_pairs={{0,4},{1,5},{2,6},{3,7},{4,8},{5,9},{6,10},{7,11},{8,12},{9,13},{1... | collective-permute-start | bytes 1179656 | tf_op jit(solution)/shard_map/ppermute | solution.py:60
  131.8 23.0 %collective-permute-start.24 = (bf16[1,256,768]{2,1,0:T(8,128)(2,1)S(1)}, bf16[1,256,768]{2,1,0:T(8,128)(2,1)S(1)}, u32[]{:S(2)}, u32[]{:S(2)}) collective-permute-start(bf16[1,256,768]{2,1,0:T(8,128)(2,1)S(1)} %get-tuple-element.136), channel_id=1, source_target_pairs={{0,12},{1,13},{2,14},{3,15},{4,0},{5,1},{6,2},{7,3},{8,4},{9,5},{1... | collective-permute-start | bytes 1179656 | tf_op jit(solution)/shard_map/ppermute | solution.py:60
  154.9 23.6 %collective-permute-start.27 = (bf16[2,256,768]{2,1,0:T(8,128)(2,1)S(1)}, bf16[2,256,768]{2,1,0:T(8,128)(2,1)}, u32[]{:S(2)}, u32[]{:S(2)}) collective-permute-start(bf16[2,256,768]{2,1,0:T(8,128)(2,1)S(1)} %get-tuple-element.148), channel_id=1, source_target_pairs={{0,4},{1,5},{2,6},{3,7},{4,8},{5,9},{6,10},{7,11},{8,12},{9,13},{1... | collective-permute-start | bytes 2359304 | tf_op jit(solution)/shard_map/ppermute | solution.py:60
  155.0 23.5 %collective-permute-start.28 = (bf16[2,256,768]{2,1,0:T(8,128)(2,1)S(1)}, bf16[2,256,768]{2,1,0:T(8,128)(2,1)S(1)}, u32[]{:S(2)}, u32[]{:S(2)}) collective-permute-start(bf16[2,256,768]{2,1,0:T(8,128)(2,1)S(1)} %get-tuple-element.151), channel_id=1, source_target_pairs={{0,12},{1,13},{2,14},{3,15},{4,0},{5,1},{6,2},{7,3},{8,4},{9,5},{1... | collective-permute-start | bytes 2359304 | tf_op jit(solution)/shard_map/ppermute | solution.py:60
  158.2 20.3 %collective-permute-start.29 = (bf16[2,2,128,768]{3,2,1,0:T(8,128)(2,1)S(1)}, bf16[2,2,128,768]{3,2,1,0:T(8,128)(2,1)}, u32[]{:S(2)}, u32[]{:S(2)}) collective-permute-start(bf16[2,2,128,768]{3,2,1,0:T(8,128)(2,1)S(1)} %get-tuple-element.152), channel_id=1, source_target_pairs={{0,1},{1,0},{2,3},{3,2},{4,5},{5,4},{6,7},{7,6},{8,9},{9,8},{10,11... | collective-permute-start | bytes 2359304 | tf_op jit(solution)/shard_map/ppermute | solution.py:60
  182.1 32.1 %collective-permute-start.35 = (bf16[1,384,768]{2,1,0:T(8,128)(2,1)}, bf16[1,384,768]{2,1,0:T(8,128)(2,1)}, u32[]{:S(2)}, u32[]{:S(2)}) collective-permute-start(bf16[1,384,768]{2,1,0:T(8,128)(2,1)} %pad_maximum_fusion.4), channel_id=1, source_target_pairs={{0,12},{1,13},{2,14},{3,15},{4,0},{5,1},{6,2},{7,3},{8,4},{9,5},{1... | collective-permute-start | bytes 1769480 | tf_op jit(solution)/shard_map/ppermute | solution.py:60
  187.9 26.3 %collective-permute-start.33 = (bf16[2,128,768]{2,1,0:T(8,128)(2,1)}, bf16[2,128,768]{2,1,0:T(8,128)(2,1)}, u32[]{:S(2)}, u32[]{:S(2)}) collective-permute-start(bf16[2,128,768]{2,1,0:T(8,128)(2,1)} %get-tuple-element.158), channel_id=1, source_target_pairs={{0,12},{1,13},{2,14},{3,15},{4,0},{5,1},{6,2},{7,3},{8,4},{9,5},{1... | collective-permute-start | bytes 1179656 | tf_op jit(solution)/shard_map/ppermute | solution.py:60
  187.9 26.3 %collective-permute-start.32 = (bf16[2,256,768]{2,1,0:T(8,128)(2,1)}, bf16[2,256,768]{2,1,0:T(8,128)(2,1)}, u32[]{:S(2)}, u32[]{:S(2)}) collective-permute-start(bf16[2,256,768]{2,1,0:T(8,128)(2,1)} %add_convert_fusion.4), channel_id=1, source_target_pairs={{0,4},{1,5},{2,6},{3,7},{4,8},{5,9},{6,10},{7,11},{8,12},{9,13},{1... | collective-permute-start | bytes 2359304 | tf_op jit(solution)/shard_map/ppermute | solution.py:60
  189.9 24.3 %collective-permute-start.34 = (bf16[2,2,128,768]{3,2,1,0:T(8,128)(2,1)}, bf16[2,2,128,768]{3,2,1,0:T(8,128)(2,1)}, u32[]{:S(2)}, u32[]{:S(2)}) collective-permute-start(bf16[2,2,128,768]{3,2,1,0:T(8,128)(2,1)} %get-tuple-element.160), channel_id=1, source_target_pairs={{0,1},{1,0},{2,3},{3,2},{4,5},{5,4},{6,7},{7,6},{8,9},{9,8},{10,11... | collective-permute-start | bytes 2359304 | tf_op jit(solution)/shard_map/ppermute | solution.py:60
  215.7 19.1 %collective-permute-start.36 = (bf16[192,2048]{1,0:T(8,128)(2,1)}, bf16[192,2048]{1,0:T(8,128)(2,1)S(1)}, u32[]{:S(2)}, u32[]{:S(2)}) collective-permute-start(bf16[192,2048]{1,0:T(8,128)(2,1)} %bitcast.14), channel_id=1, source_target_pairs={{0,3},{1,2},{2,1},{3,0},{4,7},{5,6},{6,5},{7,4},{8,11},{9,10},{10,... | collective-permute-start | bytes 2359304 | tf_op jit(solution)/shard_map/ppermute | solution.py:60
  225.3 19.4 %all-to-all-start.4 = ((bf16[4,48,2048]{2,1,0:T(8,128)(2,1)}), bf16[4,48,2048]{2,1,0:T(8,128)(2,1)S(1)}, u32[]{:S(2)}, u32[]{:S(2)}) async-start(bf16[4,48,2048]{2,1,0:T(8,128)(2,1)} %bitcast.15), calls=%async_computation.4 | async-start | bytes 1572864 | tf_op jit(solution)/shard_map/all_to_all | solution.py:63
  240.1 29.6 %collective-permute-start.40 = (bf16[192,2048]{1,0:T(8,128)(2,1)}, bf16[192,2048]{1,0:T(8,128)(2,1)}, u32[]{:S(2)}, u32[]{:S(2)}) collective-permute-start(bf16[192,2048]{1,0:T(8,128)(2,1)} %bitcast.19), channel_id=1, source_target_pairs={{0,3},{1,2},{2,1},{3,0},{4,7},{5,6},{6,5},{7,4},{8,11},{9,10},{10,... | collective-permute-start | bytes 2359304 | tf_op jit(solution)/shard_map/ppermute | solution.py:60
  (76 other events, 877.9 us)
where the time goes:
time: 279 us; the launch traced here: 278 us
  starting transfers between devices  83.5 us (30%)
  waiting for transfers between devices  76.7 us (27%)
  Pallas kernels  66.9 us (24%)
  other arithmetic  32.1 us (12%)
  local copies, waits for them, and re-layouts  17.8 us (6%)
    pallas_call x6, Pallas kernels, run(): pl.pallas_call(kernel, out_shape=shapes, in_specs=[pl.BlockSpec(memory_sp...  59.8 us
    ppermute x39, waiting for transfers between devices, send(): return self.hold(lax.ppermute(value, AXES, MOVES[link]), rounds)  58.3 us
    ppermute x39, starting transfers between devices, send(): return self.hold(lax.ppermute(value, AXES, MOVES[link]), rounds)  50.8 us
    all_to_all x7, starting transfers between devices, exchange(): lax.all_to_all(value, 'expert', split_axis=0, concat_axis=0, tiled=True,...  32.6 us
    all_to_all x7, waiting for transfers between devices, exchange(): lax.all_to_all(value, 'expert', split_axis=0, concat_axis=0, tiled=True,...  18.4 us
    convert_element_type x12, other arithmetic, add(): return sum((t.astype(F32) for t in terms)).astype(BF16)  15.7 us
    unnamed x100, local copies, waits for them, and re-layouts  10.9 us
  transfers between devices with their start and end apart: 50, of which 19 were waited for; matrix products, arithmetic and copies ran while one was open for 13% of the time, Pallas kernels for 23%

commit v1 on v0

--- a/solution.py
+++ b/solution.py
@@ -118,10 +118,11 @@
         select = jnp.concatenate(chosen, axis=0).astype(BF16)
         side = half if own else 1 - half
         for kind in range(2):
-            for step in range(4):
+
+            def fill(step, unused, own=own, kind=kind, side=side, select=select, weight=weight):
                 block = lax.rem(y + step, 4) * 2 + (side if kind == 0 else 1 - side)
                 read = pl.ds(pl.multiple_of(block * width, width), width)
-                put = slice((kind * 4 + step) * width, (kind * 4 + step + 1) * width)
+                put = pl.ds(pl.multiple_of((kind * 4 + step) * width, width), width)
                 rows = jnp.dot(select, tok_ref[:, read], preferred_element_type=F32).astype(BF16)
                 cots = jnp.dot(select, cot_ref[:, read], preferred_element_type=F32)
                 grads = (weight * cots).astype(BF16)
@@ -133,6 +134,9 @@
                 else:
                     outs[1][:, put] = rows
                     outs[2][:, put] = grads
+                return unused
+
+            lax.fori_loop(0, 4, fill, 0)
 
 
 def dispatch(place, ids, gates, tokens, cotangent):
@@ -172,13 +176,13 @@
             jnp.concatenate([s * g for s, g in zip(chosen, gate)], axis=0).astype(BF16)
         )
         chosen_of.append(chosen)
-    totals = [jnp.zeros((4 * MOST, 1), F32) for _ in range(2)]
-    for step in range(4):
+    def step_of(step, totals):
+        totals = list(totals)
         for kind in range(2):
             block = lax.rem(y + step, 4) * 2 + (half if kind == 0 else 1 - half)
             at = pl.ds(pl.multiple_of(block * width, width), width)
-            mine = slice((kind * 4 + step) * width, (kind * 4 + step + 1) * width)
-            other = slice(((1 - kind) * 4 + step) * width, ((1 - kind) * 4 + step + 1) * width)
+            mine = pl.ds(pl.multiple_of((kind * 4 + step) * width, width), width)
+            other = pl.ds(pl.multiple_of(((1 - kind) * 4 + step) * width, width), width)
             cot = cot_ref[:, at]
             outs = (own_ref[:, mine], oth_ref[:, other])
             grads = (gown_ref[:, mine], goth_ref[:, other])
@@ -193,6 +197,10 @@
             for i in range(2):
                 cots = jnp.dot(picked[i], cot, preferred_element_type=F32)
                 totals[i] += jnp.sum(cots * outs[i].astype(F32), axis=1, keepdims=True)
+        return tuple(totals)
+
+    zero = jnp.zeros((4 * MOST, 1), F32)
+    totals = lax.fori_loop(0, 4, step_of, (zero, zero))
     result = jnp.zeros(ids.shape, F32)
     for i, own in enumerate((True, False)):
         side = half if own else 1 - half
@@ -256,13 +264,6 @@
 
 def add(*terms):
     return sum(t.astype(F32) for t in terms).astype(BF16)
-
-
-def whole_width(mine, other, width, core):
-    part = mine.shape[2]
-    left = jnp.where(core == 0, mine, other)
-    right = jnp.where(core == 0, other, mine)
-    return jnp.concatenate([left, right[:, :, 2 * part - width :]], axis=2).astype(F32)
 
 
 def dot(a, b, over):
@@ -470,6 +471,67 @@
     lax.fori_loop(0, 2, grad_step, 0)
 
 
+STEP = 64
+
+
+def sum_rows(to, *terms):
+    def step(i, unused):
+        at = chunk(i, STEP)
+        to[at, :] = sum(t[at, :].astype(F32) for t in terms).astype(to.dtype)
+        return unused
+
+    lax.fori_loop(0, to.shape[0] // STEP, step, 0)
+
+
+def near_kernel(place, blk_far, blk1, keep, got_a, dn_far, mir3, own_far, own_sum, blk, mir, dn):
+    size = mir3.shape[1]
+    for g in range(2):
+        sum_rows(blk.at[g], blk_far.at[g], blk1.at[g])
+        sum_rows(mir.at[g], keep.at[2, g], got_a.at[0, g])
+    sum_rows(dn.at[0, 0:size], dn_far.at[0], mir3.at[0])
+    sum_rows(dn.at[0, size:], own_far.at[0], own_sum.at[3])
+
+
+def cross_kernel(place, blk0, blk_back, blk_near, mir0, dn_back, dn_down, *refs):
+    keep, got_a, got_b, mir_far, own_sum, stay, leave, up, down = refs
+    low = place[2]
+    rows = stay.shape[1]
+    first, second = pl.ds(low * rows, rows), pl.ds((1 - low) * rows, rows)
+    for g in range(2):
+        for to, at in ((stay, first), (leave, second)):
+            sum_rows(to.at[g], blk0.at[g, at], blk_back.at[g, at], blk_near.at[g, at])
+        sum_rows(up.at[g], keep.at[1, g], got_a.at[1, g])
+        sum_rows(down.at[g], mir_far.at[g], keep.at[3, g], got_b.at[1, g])
+    for to, at in ((stay, second), (leave, first)):
+        sum_rows(to.at[2], mir0.at[0, at], dn_back.at[0, at], dn_down.at[0, at])
+    sum_rows(up.at[2], own_sum.at[1])
+
+
+def last_kernel(place, stay, leave_got, keep, got_b, up, mir_near, own_sum, dn_down, mir, own):
+    rows = stay.shape[1]
+    for g in range(2):
+        sum_rows(mir.at[g], keep.at[0, g], got_b.at[0, g], up.at[g], mir_near.at[g])
+        sum_rows(own.at[g], stay.at[g], leave_got.at[g])
+    sum_rows(mir.at[2], stay.at[2], leave_got.at[2])
+    sum_rows(own.at[2], own_sum.at[0], up.at[2], dn_down.at[0, 2 * rows :])
+
+
+def pick_kernel(place, own, away, keep_ref, give_ref):
+    here = place[3] == place[1]
+    for i in range(3):
+        keep_ref[i] = jnp.where(here, own[i], away[i])
+        give_ref[i] = jnp.where(here, away[i], own[i])
+
+
+def widen_kernel(place, keep, got, *outs):
+    first = place[3] == 0
+    part = keep.shape[2]
+    for i, out in enumerate(outs):
+        extra = 2 * part - out.shape[2]
+        out[0, :, :part] = jnp.where(first, keep[i], got[i]).astype(F32)
+        out[0, :, part:] = jnp.where(first, got[i, :, extra:], keep[i, :, extra:]).astype(F32)
+
+
 def run(kernel, name, place, local, remote, outs, far_outs, scratch, flops):
     vmem, anywhere = pl.BlockSpec(memory_space=pltpu.VMEM), pl.BlockSpec(memory_space=pl.ANY)
     shapes = [jax.ShapeDtypeStruct(*o) for o in tuple(outs) + tuple(far_outs)]
@@ -638,43 +700,66 @@
     )
     r.hold(theirs)
     r.next()
-    blk_near = send("up", add(blk_far, blk_t1))
-    mir_far = send("down", add(mir_keep[2], got_a[0]))
+    two, three = ((2, rows, part), BF16), ((3, rows, part), BF16)
+    blk_mid, mir_mid, dn_mid = run(
+        near_kernel,
+        "near",
+        place,
+        (r.pin(blk_far), blk_t1, mir_keep, got_a, dn_far, mir_t3, own_far, own_sum),
+        (),
+        [((2, 2 * rows, part), BF16), two, ((1, 3 * rows, part), BF16)],
+        [],
+        [],
+        1,
+    )
+    blk_near = send("up", blk_mid)
+    mir_far = send("down", mir_mid)
     got_b = send("side", give_b)
-    dn_down = send(
-        "down", jnp.concatenate([add(dn_far, mir_t3), add(own_far, own_sum[3:])], axis=1)
-    )
+    dn_down = send("down", dn_mid)
     got = send("core", theirs)
     out = r.hold(add(r.late(out_mine), got[: 2 * quarter]))
     out_home = r.exchange(out[quarter:].reshape(4, MOST, depth))
     grd = r.hold(add(r.late(grad_mine), got[2 * quarter :]))
     grad_home = r.exchange(grd[quarter:].reshape(4, MOST, depth), 2)
     r.next()
-    dn_down, blk_near, blk_back = r.pin(dn_down), r.pin(blk_near), r.pin(blk_back)
-    dn_near, own_near = dn_down[:, : 2 * rows], dn_down[:, 2 * rows :]
-    mir_back = send("up", jnp.concatenate([add(mir_keep[1], got_a[1]), own_sum[1:2]], axis=0))
-    mir_near = send("down", add(r.pin(mir_far), mir_keep[3], r.pin(got_b)[1]))
-    blk = add(blk_t0, blk_back, blk_near)
-    mir_dn = add(mir_t0, dn_back, dn_near)
-    low_half, high_half = join(blk[:, :rows], mir_dn[:, rows:]), join(blk[:, rows:], mir_dn[:, :rows])
-    stay = jnp.where(low == 0, low_half, high_half)
-    leave_got = send("side", jnp.where(low == 0, high_half, low_half))
+    stay, leave, up_sum, down_sum = run(
+        cross_kernel,
+        "cross",
+        place,
+        (blk_t0, blk_back, r.pin(blk_near), mir_t0, dn_back, r.pin(dn_down), mir_keep)
+        + (got_a, got_b, mir_far, own_sum),
+        (),
+        [three, three, three, two],
+        [],
+        [],
+        1,
+    )
+    mir_back = send("up", up_sum)
+    mir_near = send("down", down_sum)
+    leave_got = send("side", leave)
     out_oth = send("mirror", out_home.reshape(quarter, depth))
     out_own = r.exchange(r.late(out[:quarter]).reshape(4, MOST, depth), 2)
     r.next()
-    here = core == side
-    mir_back = r.pin(mir_back)
-    mine = add(stay, r.pin(leave_got))
-    gu_mir = add(mir_keep[0], got_b[0], mir_back[:2], r.pin(mir_near))
-    away = send("mirror", join(gu_mir, mine[2:]))
+    mir_sum, own = run(
+        last_kernel,
+        "last",
+        place,
+        (stay, r.pin(leave_got), mir_keep, got_b, r.pin(mir_back), mir_near, own_sum, dn_down),
+        (),
+        [three, three],
+        [],
+        [],
+        1,
+    )
+    away = send("mirror", mir_sum)
     grad_oth = send("mirror", grad_home.reshape(quarter, depth))
     grad_own = r.exchange(r.late(grd[:quarter]).reshape(4, MOST, depth))
     out_own, grad_own = out_own.reshape(quarter, depth), grad_own.reshape(quarter, depth)
-    own = join(mine[:2], add(own_sum[:1], mir_back[2:], own_near))
-    other = lax.ppermute(jnp.where(here, away, own), AXES, TO_CORE)
-    kept = jnp.where(here, own, away)
-    grad_gate, grad_up, grad_down = (
-        whole_width(kept[i : i + 1], other[i : i + 1], width, core) for i in range(3)
+    kept, give = run(pick_kernel, "pick", place, (own, away), (), [three, three], [], [], 1)
+    other = lax.ppermute(give, AXES, TO_CORE)
+    wide = ((1, rows, width), F32)
+    grad_gate, grad_up, grad_down = run(
+        widen_kernel, "widen", place, (kept, other), (), [wide] * 3, [], [], 1
     )
 
     output, grad_tokens, grad_gates = combine(

time: 279 us -> 294 us (1.054)
  other arithmetic: 32.1 us -> 10.8 us
  Pallas kernels: 66.9 us -> 82.9 us
  local copies, waits for them, and re-layouts: 17.8 us -> 31.7 us
  waiting for transfers between devices: 76.7 us -> 80.7 us
    unnamed x100 -> x114, local copies, waits for them, and re-layouts: 10.9 us -> 24.9 us
    ppermute x39, waiting for transfers between devices: 58.3 us -> 71.9 us  [send(): return self.hold(lax.ppermute(value, AXES, MOVES[link]), rounds)]
    pallas_call x6 -> x11, Pallas kernels: 59.8 us -> 71.8 us  [run(): pl.pallas_call(kernel, out_shape=shapes, in_specs=[pl.BlockSpec(memory_sp...]
    convert_element_type x12 -> x2, other arithmetic: 15.7 us -> 4.39 us  [add(): return sum((t.astype(F32) for t in terms)).astype(BF16)]
    all_to_all x7, waiting for transfers between devices: 18.4 us -> 8.77 us  [exchange(): lax.all_to_all(value, 'expert', split_axis=0, concat_axis=0, tiled=True,...]
    select_n x5 -> x0, other arithmetic: 4.6 us -> none  [the longest x1 2.37 us: on_device(): other = lax.ppermute(jnp.where(here, away, own), AXES, TO_CORE)]
  transfers between devices with their start and end apart: 50 -> 50, of which waited for: 19 -> 19; matrix products, arithmetic and copies ran while one was open for 13% -> 6% of each run, Pallas kernels for 23% -> 27%
where the time goes in v1:
time: 294 us; the launch traced here: 292 us
  starting transfers between devices  85 us (29%)
  Pallas kernels  82.9 us (28%)
  waiting for transfers between devices  80.7 us (27%)
  local copies, waits for them, and re-layouts  31.7 us (11%)
  other arithmetic  10.8 us (4%)
    ppermute x39, waiting for transfers between devices, send(): return self.hold(lax.ppermute(value, AXES, MOVES[link]), rounds)  71.9 us
    pallas_call x11, Pallas kernels, run(): pl.pallas_call(kernel, out_shape=shapes, in_specs=[pl.BlockSpec(memory_sp...  71.8 us
    ppermute x39, starting transfers between devices, send(): return self.hold(lax.ppermute(value, AXES, MOVES[link]), rounds)  51.9 us
    all_to_all x7, starting transfers between devices, exchange(): lax.all_to_all(value, 'expert', split_axis=0, concat_axis=0, tiled=True,...  33 us
    unnamed x114, local copies, waits for them, and re-layouts  24.9 us
    all_to_all x7, waiting for transfers between devices, exchange(): lax.all_to_all(value, 'expert', split_axis=0, concat_axis=0, tiled=True,...  8.77 us
  transfers between devices with their start and end apart: 50, of which 19 were waited for; matrix products, arithmetic and copies ran while one was open for 6% of the time, Pallas kernels for 27%

profile of v1, /device:TPU:0, one launch (start us, length us, event | category | flops | bytes accessed | tf_op | source)
XLA Modules:
  0.0 292.0 jit_solution(15444429235774367268)
XLA Ops:
  15.0 3.9 %collective-permute-done.4.refs_9_.refs_11_ = bf16[1,128,768]{2,1,0:T(8,128)(2,1)S(1)} collective-permute-done((bf16[1,128,768]{2,1,0:T(8,128)(2,1)S(1)}, bf16[1,128,768]{2,1,0:T(8,128)(2,1)S(1)}, u32[]{:S(2)}, u32[]{:S(2)}) %collective-permute-start.4) | collective-permute-done | bytes 196640 | tf_op jit(solution)/shard_map/ppermute | solution.py:60
  18.9 3.4 %collective-permute-done.3.refs_10_.refs_12_ = bf16[1,128,768]{2,1,0:T(8,128)(2,1)S(1)} collective-permute-done((bf16[1,128,768]{2,1,0:T(8,128)(2,1)S(1)}, bf16[1,128,768]{2,1,0:T(8,128)(2,1)S(1)}, u32[]{:S(2)}, u32[]{:S(2)}) %collective-permute-start.3) | collective-permute-done | bytes 196640 | tf_op jit(solution)/shard_map/ppermute | solution.py:60
  27.1 5.5 %dispatch.1 = (bf16[384,2048]{1,0:T(8,128)(2,1)}, bf16[192,2048]{1,0:T(8,128)(2,1)S(1)}, bf16[192,2048]{1,0:T(8,128)(2,1)S(1)}) custom-call(s32[4]{0:T(128)S(1)} %pad_add_fusion.place, s32[6,256]{1,0:T(8,128)S(1)} %bitcast.19, bf16[6,256]{1,0:T(8,128)(2,1)S(1)} %bitcast.21, bf16[256,2048]{1,0:T(8,128)(2,1)S(1)} %copy-done.43, bf16[256,2048]{1,0:T(8,128)(2,1)S(1)} %copy-done.44), custom_call_target="tpu_custom_call" | custom-call | flops 1000000000 | bytes 6000000 | tf_op jit(solution)/shard_map/dispatch/pallas_call | solution.py:147
  34.4 5.3 %all-to-all-start = ((bf16[4,96,2048]{2,1,0:T(8,128)(2,1)}), bf16[4,96,2048]{2,1,0:T(8,128)(2,1)S(1)}, u32[]{:S(2)}, u32[]{:S(2)}) async-start(bf16[4,96,2048]{2,1,0:T(8,128)(2,1)} %bitcast.6), calls=%async_computation | async-start | bytes 3145728 | tf_op jit(solution)/shard_map/all_to_all | solution.py:63
  48.4 10.3 %collective-permute-done.10.refs_11_.refs_7_.refs_13_ = bf16[3,128,768]{2,1,0:T(8,128)(2,1)S(1)} collective-permute-done((bf16[3,128,768]{2,1,0:T(8,128)(2,1)S(1)}, bf16[3,128,768]{2,1,0:T(8,128)(2,1)S(1)}, u32[]{:S(2)}, u32[]{:S(2)}) %collective-permute-start.10) | collective-permute-done | bytes 589856 | tf_op jit(solution)/shard_map/ppermute | solution.py:60
  65.0 4.5 %all-to-all-start.1 = ((bf16[4,48,2048]{2,1,0:T(8,128)(2,1)}), bf16[4,48,2048]{2,1,0:T(8,128)(2,1)S(1)}, u32[]{:S(2)}, u32[]{:S(2)}) async-start(bf16[4,48,2048]{2,1,0:T(8,128)(2,1)} %bitcast.7), calls=%async_computation.1 | async-start | bytes 1572864 | tf_op jit(solution)/shard_map/all_to_all | solution.py:63
  73.9 8.6 %all-to-all-done.1.refs_1_.refs_5_ = bf16[4,48,2048]{2,1,0:T(8,128)(2,1)S(1)} async-done(((bf16[4,48,2048]{2,1,0:T(8,128)(2,1)}), bf16[4,48,2048]{2,1,0:T(8,128)(2,1)S(1)}, u32[]{:S(2)}, u32[]{:S(2)}) %all-to-all-start.1) | async-done | bytes 786464 | tf_op jit(solution)/shard_map/all_to_all | solution.py:63
  82.5 3.4 %collective-permute-done.14.refs_13_.refs_9_.refs_15_ = bf16[5,128,768]{2,1,0:T(8,128)(2,1)} collective-permute-done((bf16[5,128,768]{2,1,0:T(8,128)(2,1)}, bf16[5,128,768]{2,1,0:T(8,128)(2,1)}, u32[]{:S(2)}, u32[]{:S(2)}) %collective-permute-start.14) | collective-permute-done | bytes 983072 | tf_op jit(solution)/shard_map/ppermute | solution.py:60
  93.5 4.5 %all-to-all-start.2 = ((bf16[4,48,2048]{2,1,0:T(8,128)(2,1)}), bf16[4,48,2048]{2,1,0:T(8,128)(2,1)}, u32[]{:S(2)}, u32[]{:S(2)}) async-start(bf16[4,48,2048]{2,1,0:T(8,128)(2,1)} %bitcast.8), calls=%async_computation.2 | async-start | bytes 1572864 | tf_op jit(solution)/shard_map/all_to_all | solution.py:63
  103.9 12.6 %forward.1 = (bf16[768,768]{1,0:T(8,128)(2,1)S(1)}, f32[768,768]{1,0:T(8,128)}, f32[768,768]{1,0:T(8,128)}) custom-call(s32[4]{0:T(128)S(1)} %pad_add_fusion.place, bf16[4,96,2048]{2,1,0:T(8,128)(2,1)} %copy-done.3, bf16[4,48,2048]{2,1,0:T(8,128)(2,1)S(1)} %all-to-all-done.1.refs_1_.refs_5_, bf16[4,96,2048]{2,1,0:T(8,128)(2,1)} %collective-permute-done.16.refs_2_.refs_6_, ...), custom_call_target="tpu_custom_call" | custom-call | flops 4831838208 | bytes 17498112 | tf_op jit(solution)/shard_map/forward/pallas_call | solution.py:540
  124.7 10.0 %down_term.1 = (bf16[4,128,768]{2,1,0:T(8,128)(2,1)S(1)}, bf16[4,128,768]{2,1,0:T(8,128)(2,1)S(1)}, bf16[1,256,768]{2,1,0:T(8,128)(2,1)S(1)}, bf16[1,256,768]{2,...) custom-call(s32[4]{0:T(128)S(1)} %pad_add_fusion.place, ...), custom_call_target="tpu_custom_call" | custom-call | flops 2415919104 | bytes 9043968 | tf_op jit(solution)/shard_map/down_term/pallas_call | solution.py:540
  139.9 20.1 %gradient.1 = (bf16[2,768,768]{2,1,0:T(8,128)(2,1)}, bf16[2,256,768]{2,1,0:T(8,128)(2,1)S(1)}, bf16[2,256,768]{2,1,0:T(8,128)(2,1)S(1)}, bf16[2,256,768]{2,1,0:T...) custom-call(s32[4]{0:T(128)S(1)} %pad_add_fusion.place, ...), custom_call_target="tpu_custom_call" | custom-call | flops 7247757312 | bytes 27131904 | tf_op jit(solution)/shard_map/gradient/pallas_call | solution.py:540
  167.0 15.2 %outputs.1 = (f32[384,2048]{1,0:T(8,128)}, f32[384,2048]{1,0:T(8,128)}, bf16[768,2048]{1,0:T(8,128)(2,1)}) custom-call(s32[4]{0:T(128)S(1)} %pad_add_fusion.place, bf16[768,768]{1,0:T(8,128)(2,1)} %copy-done.52, bf16[2,768,768]{2,1,0:T(8,128)(2,1)} %get-tuple-element.156.both_ref, bf16[2,256,768]{2,1,0:T(8,128)(2,1)S(1)} %maximum_select_fusion.refs_4_.refs_0_, ...), custom_call_target="tpu_custom_call" | custom-call | flops 7247757312 | bytes 24182784 | tf_op jit(solution)/shard_map/outputs/pallas_call | solution.py:540
  187.4 3.8 %collective-permute-start.35 = (bf16[1,384,768]{2,1,0:T(8,128)(2,1)}, bf16[1,384,768]{2,1,0:T(8,128)(2,1)}, u32[]{:S(2)}, u32[]{:S(2)}) collective-permute-start(bf16[1,384,768]{2,1,0:T(8,128)(2,1)} %get-tuple-element.177), channel_id=1, source_target_pairs={{0,12},{1,13},{2,14},{3,15},{4,0},{5,1},{6,2},{7,3},{8,4},{9,5},{1... | collective-permute-start | bytes 1769480 | tf_op jit(solution)/shard_map/ppermute | solution.py:60
  192.0 4.2 %add_convert_fusion = (bf16[384,2048]{1,0:T(8,128)(2,1)}, bf16[384,2048]{1,0:T(8,128)(2,1)S(1)}) fusion(f32[384,2048]{1,0:T(8,128)} %get-tuple-element.182, bf16[768,2048]{1,0:T(8,128)(2,1)S(1)} %collective-permute-done.31, f32[384,2048]{1,0:T(8,128)S(1)} %copy-done.54), kind=kLoop, calls=%fused_computation | loop fusion | flops 4718592 | bytes 12582912 | tf_op jit(solution)/shard_map/convert_element_type | solution.py:266
  197.5 4.8 %all-to-all-start.3 = ((bf16[4,48,2048]{2,1,0:T(8,128)(2,1)}), bf16[4,48,2048]{2,1,0:T(8,128)(2,1)}, u32[]{:S(2)}, u32[]{:S(2)}) async-start(bf16[4,48,2048]{2,1,0:T(8,128)(2,1)} %bitcast.26), calls=%async_computation.3 | async-start | bytes 1572864 | tf_op jit(solution)/shard_map/all_to_all | solution.py:63
  205.5 8.3 %collective-permute-done.33.refs_3_ = bf16[2,128,768]{2,1,0:T(8,128)(2,1)S(1)} collective-permute-done((bf16[2,128,768]{2,1,0:T(8,128)(2,1)}, bf16[2,128,768]{2,1,0:T(8,128)(2,1)S(1)}, u32[]{:S(2)}, u32[]{:S(2)}) %collective-permute-start.33) | collective-permute-done | bytes 393248 | tf_op jit(solution)/shard_map/ppermute | solution.py:60
  218.6 4.6 %all-to-all-start.5 = ((bf16[4,48,2048]{2,1,0:T(8,128)(2,1)}), bf16[4,48,2048]{2,1,0:T(8,128)(2,1)}, u32[]{:S(2)}, u32[]{:S(2)}) async-start(bf16[4,48,2048]{2,1,0:T(8,128)(2,1)} %bitcast.25), calls=%async_computation.5 | async-start | bytes 1572864 | tf_op jit(solution)/shard_map/all_to_all | solution.py:63
  233.2 3.6 %collective-permute-start.39 = (bf16[2,128,768]{2,1,0:T(8,128)(2,1)}, bf16[2,128,768]{2,1,0:T(8,128)(2,1)S(1)}, u32[]{:S(2)}, u32[]{:S(2)}) collective-permute-start(bf16[2,128,768]{2,1,0:T(8,128)(2,1)} %get-tuple-element.189), channel_id=1, source_target_pairs={{0,12},{1,13},{2,14},{3,15},{4,0},{5,1},{6,2},{7,3},{8,4},{9,5},{1... | collective-permute-start | bytes 1179656 | tf_op jit(solution)/shard_map/ppermute | solution.py:60
  236.8 4.8 %all-to-all-start.4 = ((bf16[4,48,2048]{2,1,0:T(8,128)(2,1)}), bf16[4,48,2048]{2,1,0:T(8,128)(2,1)}, u32[]{:S(2)}, u32[]{:S(2)}) async-start(bf16[4,48,2048]{2,1,0:T(8,128)(2,1)} %bitcast.23), calls=%async_computation.4 | async-start | bytes 1572864 | tf_op jit(solution)/shard_map/all_to_all | solution.py:63
  256.0 4.5 %all-to-all-start.6 = ((bf16[4,48,2048]{2,1,0:T(8,128)(2,1)}), bf16[4,48,2048]{2,1,0:T(8,128)(2,1)S(1)}, u32[]{:S(2)}, u32[]{:S(2)}) async-start(bf16[4,48,2048]{2,1,0:T(8,128)(2,1)} %bitcast.24), calls=%async_computation.6 | async-start | bytes 1572864 | tf_op jit(solution)/shard_map/all_to_all | solution.py:63
  260.5 10.0 %collective-permute-done.41.away = bf16[3,128,768]{2,1,0:T(8,128)(2,1)S(1)} collective-permute-done((bf16[3,128,768]{2,1,0:T(8,128)(2,1)}, bf16[3,128,768]{2,1,0:T(8,128)(2,1)S(1)}, u32[]{:S(2)}, u32[]{:S(2)}) %collective-permute-start.41) | collective-permute-done | bytes 589856 | tf_op jit(solution)/shard_map/ppermute | solution.py:60
  272.0 11.3 %collective-permute-done.40.goth_ref = bf16[192,2048]{1,0:T(8,128)(2,1)S(1)} collective-permute-done((bf16[192,2048]{1,0:T(8,128)(2,1)}, bf16[192,2048]{1,0:T(8,128)(2,1)S(1)}, u32[]{:S(2)}, u32[]{:S(2)}) %collective-permute-start.40) | collective-permute-done | bytes 786464 | tf_op jit(solution)/shard_map/ppermute | solution.py:60
  284.5 5.5 %combine.1 = (bf16[256,2048]{1,0:T(8,128)(2,1)}, bf16[256,2048]{1,0:T(8,128)(2,1)}, f32[6,256]{1,0:T(8,128)}) custom-call(s32[4]{0:T(128)S(1)} %pad_add_fusion.place, s32[6,256]{1,0:T(8,128)S(1)} %bitcast.20, bf16[6,256]{1,0:T(8,128)(2,1)S(1)} %bitcast.22, bf16[256,2048]{1,0:T(8,128)(2,1)S(1)} %copy-done.45, bf16[192,2048]{1,0:T(8,128)(2,1)} %bitcast.12.own_ref, ...), custom_call_target="tpu_custom_call" | custom-call | flops 2000000000 | bytes 8000000 | tf_op jit(solution)/shard_map/combine/pallas_call | solution.py:217
  (217 shorter events, 118.3 us)
Async XLA Ops:
  34.4 27.6 %all-to-all-start = ((bf16[4,96,2048]{2,1,0:T(8,128)(2,1)}), bf16[4,96,2048]{2,1,0:T(8,128)(2,1)S(1)}, u32[]{:S(2)}, u32[]{:S(2)}) async-start(bf16[4,96,2048]{2,1,0:T(8,128)(2,1)} %bitcast.6), calls=%async_computation | async-start | bytes 3145728 | tf_op jit(solution)/shard_map/all_to_all | solution.py:63
  42.6 22.1 %collective-permute-start.8 = (bf16[5,128,768]{2,1,0:T(8,128)(2,1)}, bf16[5,128,768]{2,1,0:T(8,128)(2,1)}, u32[]{:S(2)}, u32[]{:S(2)}) collective-permute-start(bf16[5,128,768]{2,1,0:T(8,128)(2,1)} %pad_maximum_fusion), channel_id=1, source_target_pairs={{0,1},{1,0},{2,3},{3,2},{4,5},{5,4},{6,7},{7,6},{8,9},{9,8},{10,11... | collective-permute-start | bytes 2949128 | tf_op jit(solution)/shard_map/ppermute | solution.py:60
  42.9 19.0 %collective-permute-start.9 = (bf16[2,256,768]{2,1,0:T(8,128)(2,1)S(1)}, bf16[2,256,768]{2,1,0:T(8,128)(2,1)}, u32[]{:S(2)}, u32[]{:S(2)}) collective-permute-start(bf16[2,256,768]{2,1,0:T(8,128)(2,1)S(1)} %maximum_select_fusion.refs_4_.refs_0_), channel_id=1, source_target_pairs={{0,4},{1,5},{2,6},{3,7},{4,8},{5,9},{6,10},{7,11},{8,12},{9,13},{1... | collective-permute-start | bytes 2359304 | tf_op jit(solution)/shard_map/ppermute | solution.py:60
  64.7 21.2 %collective-permute-start.14 = (bf16[5,128,768]{2,1,0:T(8,128)(2,1)}, bf16[5,128,768]{2,1,0:T(8,128)(2,1)}, u32[]{:S(2)}, u32[]{:S(2)}) collective-permute-start(bf16[5,128,768]{2,1,0:T(8,128)(2,1)} %pad_maximum_fusion.1), channel_id=1, source_target_pairs={{0,1},{1,0},{2,3},{3,2},{4,5},{5,4},{6,7},{7,6},{8,9},{9,8},{10,11... | collective-permute-start | bytes 2949128 | tf_op jit(solution)/shard_map/ppermute | solution.py:60
  65.0 28.5 %collective-permute-start.16 = (bf16[4,96,2048]{2,1,0:T(8,128)(2,1)S(1)}, bf16[4,96,2048]{2,1,0:T(8,128)(2,1)}, u32[]{:S(2)}, u32[]{:S(2)}) collective-permute-start(bf16[4,96,2048]{2,1,0:T(8,128)(2,1)S(1)} %all-to-all-done.refs_0_.refs_4_), channel_id=1, source_target_pairs={{0,16},{1,17},{2,18},{3,19},{4,20},{5,21},{6,22},{7,23},{8,24},{9,... | collective-permute-start | bytes 4718600 | tf_op jit(solution)/shard_map/ppermute | solution.py:623
  69.5 21.3 %collective-permute-start.12 = (bf16[2,256,768]{2,1,0:T(8,128)(2,1)}, bf16[2,256,768]{2,1,0:T(8,128)(2,1)}, u32[]{:S(2)}, u32[]{:S(2)}) collective-permute-start(bf16[2,256,768]{2,1,0:T(8,128)(2,1)} %collective-permute-done.9.refs_7_.refs_3_), channel_id=1, source_target_pairs={{0,4},{1,5},{2,6},{3,7},{4,8},{5,9},{6,10},{7,11},{8,12},{9,13},{1... | collective-permute-start | bytes 2359304 | tf_op jit(solution)/shard_map/ppermute | solution.py:60
  69.9 20.9 %collective-permute-start.13 = (bf16[2,256,768]{2,1,0:T(8,128)(2,1)S(1)}, bf16[2,256,768]{2,1,0:T(8,128)(2,1)}, u32[]{:S(2)}, u32[]{:S(2)}) collective-permute-start(bf16[2,256,768]{2,1,0:T(8,128)(2,1)S(1)} %maximum_select_fusion.refs_4_.refs_0_), channel_id=1, source_target_pairs={{0,12},{1,13},{2,14},{3,15},{4,0},{5,1},{6,2},{7,3},{8,4},{9,5},{1... | collective-permute-start | bytes 2359304 | tf_op jit(solution)/shard_map/ppermute | solution.py:60
  72.8 20.7 %collective-permute-start.15 = (bf16[192,2048]{1,0:T(8,128)(2,1)}, bf16[192,2048]{1,0:T(8,128)(2,1)}, u32[]{:S(2)}, u32[]{:S(2)}) collective-permute-start(bf16[192,2048]{1,0:T(8,128)(2,1)} %copy-done.46), channel_id=1, source_target_pairs={{0,3},{1,2},{2,1},{3,0},{4,7},{5,6},{6,5},{7,4},{8,11},{9,10},{10,... | collective-permute-start | bytes 2359304 | tf_op jit(solution)/shard_map/ppermute | solution.py:60
  93.5 24.8 %all-to-all-start.2 = ((bf16[4,48,2048]{2,1,0:T(8,128)(2,1)}), bf16[4,48,2048]{2,1,0:T(8,128)(2,1)}, u32[]{:S(2)}, u32[]{:S(2)}) async-start(bf16[4,48,2048]{2,1,0:T(8,128)(2,1)} %bitcast.8), calls=%async_computation.2 | async-start | bytes 1572864 | tf_op jit(solution)/shard_map/all_to_all | solution.py:63
  98.0 20.3 %collective-permute-start.20 = (bf16[3,128,768]{2,1,0:T(8,128)(2,1)}, bf16[3,128,768]{2,1,0:T(8,128)(2,1)}, u32[]{:S(2)}, u32[]{:S(2)}) collective-permute-start(bf16[3,128,768]{2,1,0:T(8,128)(2,1)} %get-tuple-element.134), channel_id=1, source_target_pairs={{0,1},{1,0},{2,3},{3,2},{4,5},{5,4},{6,7},{7,6},{8,9},{9,8},{10,11... | collective-permute-start | bytes 1769480 | tf_op jit(solution)/shard_map/ppermute | solution.py:60
  98.8 18.7 %collective-permute-start.19 = (bf16[1,256,768]{2,1,0:T(8,128)(2,1)}, bf16[1,256,768]{2,1,0:T(8,128)(2,1)S(1)}, u32[]{:S(2)}, u32[]{:S(2)}) collective-permute-start(bf16[1,256,768]{2,1,0:T(8,128)(2,1)} %maximum_select_fusion.1.refs_14_.refs_16_), channel_id=1, source_target_pairs={{0,12},{1,13},{2,14},{3,15},{4,0},{5,1},{6,2},{7,3},{8,4},{9,5},{1... | collective-permute-start | bytes 1179656 | tf_op jit(solution)/shard_map/ppermute | solution.py:60
  135.4 26.2 %collective-permute-start.26 = (bf16[4,128,768]{2,1,0:T(8,128)(2,1)S(1)}, bf16[4,128,768]{2,1,0:T(8,128)(2,1)S(1)}, u32[]{:S(2)}, u32[]{:S(2)}) collective-permute-start(bf16[4,128,768]{2,1,0:T(8,128)(2,1)S(1)} %get-tuple-element.150), channel_id=1, source_target_pairs={{0,1},{1,0},{2,3},{3,2},{4,5},{5,4},{6,7},{7,6},{8,9},{9,8},{10,11... | collective-permute-start | bytes 2359304 | tf_op jit(solution)/shard_map/ppermute | solution.py:60
  136.6 24.2 %collective-permute-start.25 = (bf16[1,256,768]{2,1,0:T(8,128)(2,1)S(1)}, bf16[1,256,768]{2,1,0:T(8,128)(2,1)S(1)}, u32[]{:S(2)}, u32[]{:S(2)}) collective-permute-start(bf16[1,256,768]{2,1,0:T(8,128)(2,1)S(1)} %get-tuple-element.149), channel_id=1, source_target_pairs={{0,4},{1,5},{2,6},{3,7},{4,8},{5,9},{6,10},{7,11},{8,12},{9,13},{1... | collective-permute-start | bytes 1179656 | tf_op jit(solution)/shard_map/ppermute | solution.py:60
  136.7 25.0 %collective-permute-start.24 = (bf16[1,256,768]{2,1,0:T(8,128)(2,1)S(1)}, bf16[1,256,768]{2,1,0:T(8,128)(2,1)S(1)}, u32[]{:S(2)}, u32[]{:S(2)}) collective-permute-start(bf16[1,256,768]{2,1,0:T(8,128)(2,1)S(1)} %get-tuple-element.147), channel_id=1, source_target_pairs={{0,12},{1,13},{2,14},{3,15},{4,0},{5,1},{6,2},{7,3},{8,4},{9,5},{1... | collective-permute-start | bytes 1179656 | tf_op jit(solution)/shard_map/ppermute | solution.py:60
  161.6 23.5 %collective-permute-start.27 = (bf16[2,256,768]{2,1,0:T(8,128)(2,1)S(1)}, bf16[2,256,768]{2,1,0:T(8,128)(2,1)S(1)}, u32[]{:S(2)}, u32[]{:S(2)}) collective-permute-start(bf16[2,256,768]{2,1,0:T(8,128)(2,1)S(1)} %get-tuple-element.159), channel_id=1, source_target_pairs={{0,4},{1,5},{2,6},{3,7},{4,8},{5,9},{6,10},{7,11},{8,12},{9,13},{1... | collective-permute-start | bytes 2359304 | tf_op jit(solution)/shard_map/ppermute | solution.py:60
  161.6 23.5 %collective-permute-start.28 = (bf16[2,256,768]{2,1,0:T(8,128)(2,1)S(1)}, bf16[2,256,768]{2,1,0:T(8,128)(2,1)S(1)}, u32[]{:S(2)}, u32[]{:S(2)}) collective-permute-start(bf16[2,256,768]{2,1,0:T(8,128)(2,1)S(1)} %get-tuple-element.161), channel_id=1, source_target_pairs={{0,12},{1,13},{2,14},{3,15},{4,0},{5,1},{6,2},{7,3},{8,4},{9,5},{1... | collective-permute-start | bytes 2359304 | tf_op jit(solution)/shard_map/ppermute | solution.py:60
  164.9 20.3 %collective-permute-start.29 = (bf16[2,2,128,768]{3,2,1,0:T(8,128)(2,1)S(1)}, bf16[2,2,128,768]{3,2,1,0:T(8,128)(2,1)S(1)}, u32[]{:S(2)}, u32[]{:S(2)}) collective-permute-start(bf16[2,2,128,768]{3,2,1,0:T(8,128)(2,1)S(1)} %get-tuple-element.162), channel_id=1, source_target_pairs={{0,1},{1,0},{2,3},{3,2},{4,5},{5,4},{6,7},{7,6},{8,9},{9,8},{10,11... | collective-permute-start | bytes 2359304 | tf_op jit(solution)/shard_map/ppermute | solution.py:60
  165.9 19.3 %collective-permute-start.30 = (bf16[1,128,768]{2,1,0:T(8,128)(2,1)S(1)}, bf16[1,128,768]{2,1,0:T(8,128)(2,1)S(1)}, u32[]{:S(2)}, u32[]{:S(2)}) collective-permute-start(bf16[1,128,768]{2,1,0:T(8,128)(2,1)S(1)} %slice.41), channel_id=1, source_target_pairs={{0,12},{1,13},{2,14},{3,15},{4,0},{5,1},{6,2},{7,3},{8,4},{9,5},{1... | collective-permute-start | bytes 589832 | tf_op jit(solution)/shard_map/ppermute | solution.py:60
  187.4 27.1 %collective-permute-start.35 = (bf16[1,384,768]{2,1,0:T(8,128)(2,1)}, bf16[1,384,768]{2,1,0:T(8,128)(2,1)}, u32[]{:S(2)}, u32[]{:S(2)}) collective-permute-start(bf16[1,384,768]{2,1,0:T(8,128)(2,1)} %get-tuple-element.177), channel_id=1, source_target_pairs={{0,12},{1,13},{2,14},{3,15},{4,0},{5,1},{6,2},{7,3},{8,4},{9,5},{1... | collective-permute-start | bytes 1769480 | tf_op jit(solution)/shard_map/ppermute | solution.py:60
  191.2 23.4 %collective-permute-start.32 = (bf16[2,256,768]{2,1,0:T(8,128)(2,1)}, bf16[2,256,768]{2,1,0:T(8,128)(2,1)}, u32[]{:S(2)}, u32[]{:S(2)}) collective-permute-start(bf16[2,256,768]{2,1,0:T(8,128)(2,1)} %get-tuple-element.171), channel_id=1, source_target_pairs={{0,4},{1,5},{2,6},{3,7},{4,8},{5,9},{6,10},{7,11},{8,12},{9,13},{1... | collective-permute-start | bytes 2359304 | tf_op jit(solution)/shard_map/ppermute | solution.py:60
  191.2 23.4 %collective-permute-start.34 = (bf16[2,2,128,768]{3,2,1,0:T(8,128)(2,1)}, bf16[2,2,128,768]{3,2,1,0:T(8,128)(2,1)S(1)}, u32[]{:S(2)}, u32[]{:S(2)}) collective-permute-start(bf16[2,2,128,768]{3,2,1,0:T(8,128)(2,1)} %get-tuple-element.175), channel_id=1, source_target_pairs={{0,1},{1,0},{2,3},{3,2},{4,5},{5,4},{6,7},{7,6},{8,9},{9,8},{10,11... | collective-permute-start | bytes 2359304 | tf_op jit(solution)/shard_map/ppermute | solution.py:60
  214.7 33.5 %collective-permute-start.36 = (bf16[192,2048]{1,0:T(8,128)(2,1)}, bf16[192,2048]{1,0:T(8,128)(2,1)}, u32[]{:S(2)}, u32[]{:S(2)}) collective-permute-start(bf16[192,2048]{1,0:T(8,128)(2,1)} %bitcast.10), channel_id=1, source_target_pairs={{0,3},{1,2},{2,1},{3,0},{4,7},{5,6},{6,5},{7,4},{8,11},{9,10},{10,... | collective-permute-start | bytes 2359304 | tf_op jit(solution)/shard_map/ppermute | solution.py:60
  236.8 19.2 %all-to-all-start.4 = ((bf16[4,48,2048]{2,1,0:T(8,128)(2,1)}), bf16[4,48,2048]{2,1,0:T(8,128)(2,1)}, u32[]{:S(2)}, u32[]{:S(2)}) async-start(bf16[4,48,2048]{2,1,0:T(8,128)(2,1)} %bitcast.23), calls=%async_computation.4 | async-start | bytes 1572864 | tf_op jit(solution)/shard_map/all_to_all | solution.py:63
  254.9 28.4 %collective-permute-start.40 = (bf16[192,2048]{1,0:T(8,128)(2,1)}, bf16[192,2048]{1,0:T(8,128)(2,1)S(1)}, u32[]{:S(2)}, u32[]{:S(2)}) collective-permute-start(bf16[192,2048]{1,0:T(8,128)(2,1)} %bitcast.14), channel_id=1, source_target_pairs={{0,3},{1,2},{2,1},{3,0},{4,7},{5,6},{6,5},{7,4},{8,11},{9,10},{10,... | collective-permute-start | bytes 2359304 | tf_op jit(solution)/shard_map/ppermute | solution.py:60
  (83 other events, 868.7 us)

commit v2 on v0

--- a/solution.py
+++ b/solution.py
@@ -258,13 +258,6 @@
     return sum(t.astype(F32) for t in terms).astype(BF16)
 
 
-def whole_width(mine, other, width, core):
-    part = mine.shape[2]
-    left = jnp.where(core == 0, mine, other)
-    right = jnp.where(core == 0, other, mine)
-    return jnp.concatenate([left, right[:, :, 2 * part - width :]], axis=2).astype(F32)
-
-
 def dot(a, b, over):
     return lax.dot_general(a, b, (over, ((), ())), preferred_element_type=F32)
 
@@ -470,6 +463,37 @@
     lax.fori_loop(0, 2, grad_step, 0)
 
 
+STEP = 64
+
+
+def sum_rows(to, *terms):
+    def step(i, unused):
+        at = chunk(i, STEP)
+        to[at, :] = sum(t[at, :].astype(F32) for t in terms).astype(to.dtype)
+        return unused
+
+    lax.fori_loop(0, to.shape[0] // STEP, step, 0)
+
+
+def near_kernel(place, blk_far, blk1, keep, got_a, dn_far, mir3, own_far, own_sum, blk, both):
+    rows = both.shape[1]
+    for g in range(2):
+        sum_rows(blk.at[g], blk_far.at[g], blk1.at[g])
+        sum_rows(both.at[g], keep.at[2, g], got_a.at[0, g])
+        at = slice(g * rows, (g + 1) * rows)
+        sum_rows(both.at[2 + g], dn_far.at[0, at], mir3.at[0, at])
+    sum_rows(both.at[4], own_far.at[0], own_sum.at[3])
+
+
+def widen_kernel(place, keep, got, *outs):
+    first = place[3] == 0
+    part = keep.shape[2]
+    for i, out in enumerate(outs):
+        extra = 2 * part - out.shape[2]
+        out[0, :, :part] = jnp.where(first, keep[i], got[i]).astype(F32)
+        out[0, :, part:] = jnp.where(first, got[i, :, extra:], keep[i, :, extra:]).astype(F32)
+
+
 def run(kernel, name, place, local, remote, outs, far_outs, scratch, flops):
     vmem, anywhere = pl.BlockSpec(memory_space=pltpu.VMEM), pl.BlockSpec(memory_space=pl.ANY)
     shapes = [jax.ShapeDtypeStruct(*o) for o in tuple(outs) + tuple(far_outs)]
@@ -638,22 +662,31 @@
     )
     r.hold(theirs)
     r.next()
-    blk_near = send("up", add(blk_far, blk_t1))
-    mir_far = send("down", add(mir_keep[2], got_a[0]))
+    blk_mid, both_mid = run(
+        near_kernel,
+        "near",
+        place,
+        (r.pin(blk_far), blk_t1, mir_keep, got_a, dn_far, mir_t3, own_far, own_sum),
+        (),
+        [((2, 2 * rows, part), BF16), ((5, rows, part), BF16)],
+        [],
+        [],
+        1,
+    )
+    blk_near = send("up", blk_mid)
     got_b = send("side", give_b)
-    dn_down = send(
-        "down", jnp.concatenate([add(dn_far, mir_t3), add(own_far, own_sum[3:])], axis=1)
-    )
+    both_far = send("down", both_mid)
     got = send("core", theirs)
     out = r.hold(add(r.late(out_mine), got[: 2 * quarter]))
     out_home = r.exchange(out[quarter:].reshape(4, MOST, depth))
     grd = r.hold(add(r.late(grad_mine), got[2 * quarter :]))
     grad_home = r.exchange(grd[quarter:].reshape(4, MOST, depth), 2)
     r.next()
-    dn_down, blk_near, blk_back = r.pin(dn_down), r.pin(blk_near), r.pin(blk_back)
-    dn_near, own_near = dn_down[:, : 2 * rows], dn_down[:, 2 * rows :]
+    both_far, blk_near, blk_back = r.pin(both_far), r.pin(blk_near), r.pin(blk_back)
+    mir_far, own_near = both_far[:2], both_far[4:]
+    dn_near = both_far[2:4].reshape(1, 2 * rows, part)
     mir_back = send("up", jnp.concatenate([add(mir_keep[1], got_a[1]), own_sum[1:2]], axis=0))
-    mir_near = send("down", add(r.pin(mir_far), mir_keep[3], r.pin(got_b)[1]))
+    mir_near = send("down", add(mir_far, mir_keep[3], r.pin(got_b)[1]))
     blk = add(blk_t0, blk_back, blk_near)
     mir_dn = add(mir_t0, dn_back, dn_near)
     low_half, high_half = join(blk[:, :rows], mir_dn[:, rows:]), join(blk[:, rows:], mir_dn[:, :rows])
@@ -673,12 +706,13 @@
     own = join(mine[:2], add(own_sum[:1], mir_back[2:], own_near))
     other = lax.ppermute(jnp.where(here, away, own), AXES, TO_CORE)
     kept = jnp.where(here, own, away)
-    grad_gate, grad_up, grad_down = (
-        whole_width(kept[i : i + 1], other[i : i + 1], width, core) for i in range(3)
+    wide = ((1, rows, width), F32)
+    grad_gate, grad_up, grad_down = run(
+        widen_kernel, "widen", place, (kept, other), (), [wide] * 3, [], [], 1
     )
 
     output, grad_tokens, grad_gates = combine(
-        place, ids, gates, cotangent, out_own, out_oth, grad_own, grad_oth
+        after(place, grad_down), ids, gates, cotangent, out_own, out_oth, grad_own, grad_oth
     )
     return (output, grad_tokens, grad_gates.T, grad_gate, grad_up, grad_down)
 

time: 279 us -> 283 us (1.014)
  other arithmetic: 32.1 us -> 20.5 us
  local copies, waits for them, and re-layouts: 17.8 us -> 26.1 us
  waiting for transfers between devices: 76.7 us -> 81 us
  Pallas kernels: 66.9 us -> 70.8 us
    all_to_all x7, waiting for transfers between devices: 18.4 us -> 28.4 us  [exchange(): lax.all_to_all(value, 'expert', split_axis=0, concat_axis=0, tiled=True,...]
    unnamed x100 -> x112, local copies, waits for them, and re-layouts: 10.9 us -> 17.4 us
    ppermute x39 -> x38, waiting for transfers between devices: 58.3 us -> 52.6 us  [send(): return self.hold(lax.ppermute(value, AXES, MOVES[link]), rounds)]
    convert_element_type x12 -> x9, other arithmetic: 15.7 us -> 10.4 us  [add(): return sum((t.astype(F32) for t in terms)).astype(BF16)]
    pallas_call x6 -> x8, Pallas kernels: 59.8 us -> 63.7 us  [run(): pl.pallas_call(kernel, out_shape=shapes, in_specs=[pl.BlockSpec(memory_sp...]
    ppermute x39 -> x38, starting transfers between devices: 50.8 us -> 49.1 us  [send(): return self.hold(lax.ppermute(value, AXES, MOVES[link]), rounds)]
  transfers between devices with their start and end apart: 50 -> 49, of which waited for: 19 -> 19; matrix products, arithmetic and copies ran while one was open for 13% -> 9% of each run, Pallas kernels for 23% -> 23%
where the time goes in v2:
time: 283 us; the launch traced here: 281 us
  starting transfers between devices  81.7 us (29%)
  waiting for transfers between devices  81 us (29%)
  Pallas kernels  70.8 us (25%)
  local copies, waits for them, and re-layouts  26.1 us (9%)
  other arithmetic  20.5 us (7%)
    pallas_call x8, Pallas kernels, run(): pl.pallas_call(kernel, out_shape=shapes, in_specs=[pl.BlockSpec(memory_sp...  63.7 us
    ppermute x38, waiting for transfers between devices, send(): return self.hold(lax.ppermute(value, AXES, MOVES[link]), rounds)  52.6 us
    ppermute x38, starting transfers between devices, send(): return self.hold(lax.ppermute(value, AXES, MOVES[link]), rounds)  49.1 us
    all_to_all x7, starting transfers between devices, exchange(): lax.all_to_all(value, 'expert', split_axis=0, concat_axis=0, tiled=True,...  32.5 us
    all_to_all x7, waiting for transfers between devices, exchange(): lax.all_to_all(value, 'expert', split_axis=0, concat_axis=0, tiled=True,...  28.4 us
    unnamed x112, local copies, waits for them, and re-layouts  17.4 us
    convert_element_type x9, other arithmetic, add(): return sum((t.astype(F32) for t in terms)).astype(BF16)  10.4 us
  transfers between devices with their start and end apart: 49, of which 19 were waited for; matrix products, arithmetic and copies ran while one was open for 9% of the time, Pallas kernels for 23%

profile of v2, /device:TPU:0, one launch (start us, length us, event | category | flops | bytes accessed | tf_op | source)
XLA Modules:
  0.0 281.3 jit_solution(6497856258608147090)
XLA Ops:
  14.4 3.9 %collective-permute-done.4.refs_9_.refs_11_ = bf16[1,128,768]{2,1,0:T(8,128)(2,1)S(1)} collective-permute-done((bf16[1,128,768]{2,1,0:T(8,128)(2,1)S(1)}, bf16[1,128,768]{2,1,0:T(8,128)(2,1)S(1)}, u32[]{:S(2)}, u32[]{:S(2)}) %collective-permute-start.4) | collective-permute-done | bytes 196640 | tf_op jit(solution)/shard_map/ppermute | solution.py:60
  18.3 3.4 %collective-permute-done.3.refs_10_.refs_12_ = bf16[1,128,768]{2,1,0:T(8,128)(2,1)S(1)} collective-permute-done((bf16[1,128,768]{2,1,0:T(8,128)(2,1)S(1)}, bf16[1,128,768]{2,1,0:T(8,128)(2,1)S(1)}, u32[]{:S(2)}, u32[]{:S(2)}) %collective-permute-start.3) | collective-permute-done | bytes 196640 | tf_op jit(solution)/shard_map/ppermute | solution.py:60
  31.1 5.3 %all-to-all-start = ((bf16[4,96,2048]{2,1,0:T(8,128)(2,1)}), bf16[4,96,2048]{2,1,0:T(8,128)(2,1)S(1)}, u32[]{:S(2)}, u32[]{:S(2)}) async-start(bf16[4,96,2048]{2,1,0:T(8,128)(2,1)} %bitcast.6), calls=%async_computation | async-start | bytes 3145728 | tf_op jit(solution)/shard_map/all_to_all | solution.py:63
  44.0 10.3 %collective-permute-done.10.refs_11_.refs_7_.refs_13_ = bf16[3,128,768]{2,1,0:T(8,128)(2,1)S(1)} collective-permute-done((bf16[3,128,768]{2,1,0:T(8,128)(2,1)S(1)}, bf16[3,128,768]{2,1,0:T(8,128)(2,1)S(1)}, u32[]{:S(2)}, u32[]{:S(2)}) %collective-permute-start.10) | collective-permute-done | bytes 589856 | tf_op jit(solution)/shard_map/ppermute | solution.py:60
  60.7 4.5 %all-to-all-start.1 = ((bf16[4,48,2048]{2,1,0:T(8,128)(2,1)}), bf16[4,48,2048]{2,1,0:T(8,128)(2,1)S(1)}, u32[]{:S(2)}, u32[]{:S(2)}) async-start(bf16[4,48,2048]{2,1,0:T(8,128)(2,1)} %bitcast.7), calls=%async_computation.1 | async-start | bytes 1572864 | tf_op jit(solution)/shard_map/all_to_all | solution.py:63
  69.6 8.6 %all-to-all-done.1.refs_1_.refs_5_ = bf16[4,48,2048]{2,1,0:T(8,128)(2,1)S(1)} async-done(((bf16[4,48,2048]{2,1,0:T(8,128)(2,1)}), bf16[4,48,2048]{2,1,0:T(8,128)(2,1)S(1)}, u32[]{:S(2)}, u32[]{:S(2)}) %all-to-all-start.1) | async-done | bytes 786464 | tf_op jit(solution)/shard_map/all_to_all | solution.py:63
  78.2 3.4 %collective-permute-done.14.refs_13_.refs_9_.refs_15_ = bf16[5,128,768]{2,1,0:T(8,128)(2,1)} collective-permute-done((bf16[5,128,768]{2,1,0:T(8,128)(2,1)}, bf16[5,128,768]{2,1,0:T(8,128)(2,1)}, u32[]{:S(2)}, u32[]{:S(2)}) %collective-permute-start.14) | collective-permute-done | bytes 983072 | tf_op jit(solution)/shard_map/ppermute | solution.py:60
  89.1 4.5 %all-to-all-start.2 = ((bf16[4,48,2048]{2,1,0:T(8,128)(2,1)}), bf16[4,48,2048]{2,1,0:T(8,128)(2,1)}, u32[]{:S(2)}, u32[]{:S(2)}) async-start(bf16[4,48,2048]{2,1,0:T(8,128)(2,1)} %bitcast.8), calls=%async_computation.2 | async-start | bytes 1572864 | tf_op jit(solution)/shard_map/all_to_all | solution.py:63
  100.6 12.4 %forward.1 = (bf16[768,768]{1,0:T(8,128)(2,1)S(1)}, f32[768,768]{1,0:T(8,128)}, f32[768,768]{1,0:T(8,128)}) custom-call(s32[4]{0:T(128)S(1)} %pad_add_fusion.place, bf16[4,96,2048]{2,1,0:T(8,128)(2,1)} %copy-done.1, bf16[4,48,2048]{2,1,0:T(8,128)(2,1)S(1)} %all-to-all-done.1.refs_1_.refs_5_, bf16[4,96,2048]{2,1,0:T(8,128)(2,1)} %collective-permute-done.16.refs_2_.refs_6_, ...), custom_call_target="tpu_custom_call" | custom-call | flops 4831838208 | bytes 17498112 | tf_op jit(solution)/shard_map/forward/pallas_call | solution.py:502
  121.4 10.0 %down_term.1 = (bf16[4,128,768]{2,1,0:T(8,128)(2,1)S(1)}, bf16[4,128,768]{2,1,0:T(8,128)(2,1)S(1)}, bf16[1,256,768]{2,1,0:T(8,128)(2,1)S(1)}, bf16[1,256,768]{2,...) custom-call(s32[4]{0:T(128)S(1)} %pad_add_fusion.place, ...), custom_call_target="tpu_custom_call" | custom-call | flops 2415919104 | bytes 9043968 | tf_op jit(solution)/shard_map/down_term/pallas_call | solution.py:502
  133.4 3.2 %collective-permute-start.24 = (bf16[1,256,768]{2,1,0:T(8,128)(2,1)S(1)}, bf16[1,256,768]{2,1,0:T(8,128)(2,1)S(1)}, u32[]{:S(2)}, u32[]{:S(2)}) collective-permute-start(bf16[1,256,768]{2,1,0:T(8,128)(2,1)S(1)} %get-tuple-element.146), channel_id=1, source_target_pairs={{0,12},{1,13},{2,14},{3,15},{4,0},{5,1},{6,2},{7,3},{8,4},{9,5},{1... | collective-permute-start | bytes 1179656 | tf_op jit(solution)/shard_map/ppermute | solution.py:60
  136.7 20.2 %gradient.1 = (bf16[2,768,768]{2,1,0:T(8,128)(2,1)}, bf16[2,256,768]{2,1,0:T(8,128)(2,1)S(1)}, bf16[2,256,768]{2,1,0:T(8,128)(2,1)S(1)}, bf16[2,256,768]{2,1,0:T...) custom-call(s32[4]{0:T(128)S(1)} %pad_add_fusion.place, ...), custom_call_target="tpu_custom_call" | custom-call | flops 7247757312 | bytes 27131904 | tf_op jit(solution)/shard_map/gradient/pallas_call | solution.py:502
  163.9 15.2 %outputs.1 = (f32[384,2048]{1,0:T(8,128)}, f32[384,2048]{1,0:T(8,128)}, bf16[768,2048]{1,0:T(8,128)(2,1)}) custom-call(s32[4]{0:T(128)S(1)} %pad_add_fusion.place, bf16[768,768]{1,0:T(8,128)(2,1)} %copy-done.44, bf16[2,768,768]{2,1,0:T(8,128)(2,1)} %get-tuple-element.158.both_ref, bf16[2,256,768]{2,1,0:T(8,128)(2,1)S(1)} %maximum_select_fusion.refs_4_.refs_0_, ...), custom_call_target="tpu_custom_call" | custom-call | flops 7247757312 | bytes 24182784 | tf_op jit(solution)/shard_map/outputs/pallas_call | solution.py:502
  184.0 3.2 %collective-permute-start.33 = (bf16[5,128,768]{2,1,0:T(8,128)(2,1)}, bf16[5,128,768]{2,1,0:T(8,128)(2,1)}, u32[]{:S(2)}, u32[]{:S(2)}) collective-permute-start(bf16[5,128,768]{2,1,0:T(8,128)(2,1)} %get-tuple-element.169), channel_id=1, source_target_pairs={{0,12},{1,13},{2,14},{3,15},{4,0},{5,1},{6,2},{7,3},{8,4},{9,5},{1... | collective-permute-start | bytes 2949128 | tf_op jit(solution)/shard_map/ppermute | solution.py:60
  190.9 4.9 %all-to-all-start.3 = ((bf16[4,48,2048]{2,1,0:T(8,128)(2,1)}), bf16[4,48,2048]{2,1,0:T(8,128)(2,1)}, u32[]{:S(2)}, u32[]{:S(2)}) async-start(bf16[4,48,2048]{2,1,0:T(8,128)(2,1)} %bitcast.9), calls=%async_computation.3 | async-start | bytes 1572864 | tf_op jit(solution)/shard_map/all_to_all | solution.py:63
  199.4 8.6 %all-to-all-done.3 = bf16[4,48,2048]{2,1,0:T(8,128)(2,1)} async-done(((bf16[4,48,2048]{2,1,0:T(8,128)(2,1)}), bf16[4,48,2048]{2,1,0:T(8,128)(2,1)}, u32[]{:S(2)}, u32[]{:S(2)}) %all-to-all-start.3) | async-done | bytes 786464 | tf_op jit(solution)/shard_map/all_to_all | solution.py:63
  208.1 4.2 %all-to-all-start.4 = ((bf16[4,48,2048]{2,1,0:T(8,128)(2,1)}), bf16[4,48,2048]{2,1,0:T(8,128)(2,1)}, u32[]{:S(2)}, u32[]{:S(2)}) async-start(bf16[4,48,2048]{2,1,0:T(8,128)(2,1)} %bitcast.44), calls=%async_computation.4 | async-start | bytes 1572864 | tf_op jit(solution)/shard_map/all_to_all | solution.py:63
  220.1 3.2 %collective-permute-start.37 = (bf16[2,128,768]{2,1,0:T(8,128)(2,1)}, bf16[2,128,768]{2,1,0:T(8,128)(2,1)}, u32[]{:S(2)}, u32[]{:S(2)}) collective-permute-start(bf16[2,128,768]{2,1,0:T(8,128)(2,1)} %fusion), channel_id=1, source_target_pairs={{0,12},{1,13},{2,14},{3,15},{4,0},{5,1},{6,2},{7,3},{8,4},{9,5},{1... | collective-permute-start | bytes 1179656 | tf_op jit(solution)/shard_map/ppermute | solution.py:60
  223.6 6.4 %collective-permute-done.37 = bf16[2,128,768]{2,1,0:T(8,128)(2,1)} collective-permute-done((bf16[2,128,768]{2,1,0:T(8,128)(2,1)}, bf16[2,128,768]{2,1,0:T(8,128)(2,1)}, u32[]{:S(2)}, u32[]{:S(2)}) %collective-permute-start.37) | collective-permute-done | bytes 393248 | tf_op jit(solution)/shard_map/ppermute | solution.py:60
  239.6 4.6 %all-to-all-start.5 = ((bf16[4,48,2048]{2,1,0:T(8,128)(2,1)}), bf16[4,48,2048]{2,1,0:T(8,128)(2,1)S(1)}, u32[]{:S(2)}, u32[]{:S(2)}) async-start(bf16[4,48,2048]{2,1,0:T(8,128)(2,1)} %bitcast.43), calls=%async_computation.5 | async-start | bytes 1572864 | tf_op jit(solution)/shard_map/all_to_all | solution.py:63
  247.4 8.9 %collective-permute-done.39 = bf16[3,128,768]{2,1,0:T(8,128)(2,1)} collective-permute-done((bf16[3,128,768]{2,1,0:T(8,128)(2,1)}, bf16[3,128,768]{2,1,0:T(8,128)(2,1)}, u32[]{:S(2)}, u32[]{:S(2)}) %collective-permute-start.39) | collective-permute-done | bytes 589856 | tf_op jit(solution)/shard_map/ppermute | solution.py:60
  258.3 4.5 %all-to-all-start.6 = ((bf16[4,48,2048]{2,1,0:T(8,128)(2,1)}), bf16[4,48,2048]{2,1,0:T(8,128)(2,1)S(1)}, u32[]{:S(2)}, u32[]{:S(2)}) async-start(bf16[4,48,2048]{2,1,0:T(8,128)(2,1)} %bitcast.42), calls=%async_computation.6 | async-start | bytes 1572864 | tf_op jit(solution)/shard_map/all_to_all | solution.py:63
  264.8 10.9 %all-to-all-done.6 = bf16[4,48,2048]{2,1,0:T(8,128)(2,1)S(1)} async-done(((bf16[4,48,2048]{2,1,0:T(8,128)(2,1)}), bf16[4,48,2048]{2,1,0:T(8,128)(2,1)S(1)}, u32[]{:S(2)}, u32[]{:S(2)}) %all-to-all-start.6) | async-done | bytes 786464 | tf_op jit(solution)/shard_map/all_to_all | solution.py:63
  277.0 4.4 %combine.1 = (bf16[256,2048]{1,0:T(8,128)(2,1)}, bf16[256,2048]{1,0:T(8,128)(2,1)}, f32[6,256]{1,0:T(8,128)}) custom-call(s32[4]{0:T(128)S(1)} %pad_add_fusion.place, s32[6,256]{1,0:T(8,128)S(1)} %bitcast.39, bf16[6,256]{1,0:T(8,128)(2,1)S(1)} %bitcast.41, bf16[256,2048]{1,0:T(8,128)(2,1)S(1)} %copy-done.35, bf16[192,2048]{1,0:T(8,128)(2,1)S(1)} %bitcast.36, ...), custom_call_target="tpu_custom_call" | custom-call | flops 2000000000 | bytes 8000000 | tf_op jit(solution)/shard_map/combine/pallas_call | solution.py:209
  (227 shorter events, 111.3 us)
Async XLA Ops:
  31.1 27.3 %all-to-all-start = ((bf16[4,96,2048]{2,1,0:T(8,128)(2,1)}), bf16[4,96,2048]{2,1,0:T(8,128)(2,1)S(1)}, u32[]{:S(2)}, u32[]{:S(2)}) async-start(bf16[4,96,2048]{2,1,0:T(8,128)(2,1)} %bitcast.6), calls=%async_computation | async-start | bytes 3145728 | tf_op jit(solution)/shard_map/all_to_all | solution.py:63
  38.3 22.1 %collective-permute-start.8 = (bf16[5,128,768]{2,1,0:T(8,128)(2,1)}, bf16[5,128,768]{2,1,0:T(8,128)(2,1)}, u32[]{:S(2)}, u32[]{:S(2)}) collective-permute-start(bf16[5,128,768]{2,1,0:T(8,128)(2,1)} %pad_maximum_fusion), channel_id=1, source_target_pairs={{0,1},{1,0},{2,3},{3,2},{4,5},{5,4},{6,7},{7,6},{8,9},{9,8},{10,11... | collective-permute-start | bytes 2949128 | tf_op jit(solution)/shard_map/ppermute | solution.py:60
  38.6 18.9 %collective-permute-start.9 = (bf16[2,256,768]{2,1,0:T(8,128)(2,1)S(1)}, bf16[2,256,768]{2,1,0:T(8,128)(2,1)S(1)}, u32[]{:S(2)}, u32[]{:S(2)}) collective-permute-start(bf16[2,256,768]{2,1,0:T(8,128)(2,1)S(1)} %maximum_select_fusion.refs_4_.refs_0_), channel_id=1, source_target_pairs={{0,4},{1,5},{2,6},{3,7},{4,8},{5,9},{6,10},{7,11},{8,12},{9,13},{1... | collective-permute-start | bytes 2359304 | tf_op jit(solution)/shard_map/ppermute | solution.py:60
  39.2 19.2 %collective-permute-start.11 = (bf16[192,2048]{1,0:T(8,128)(2,1)S(1)}, bf16[192,2048]{1,0:T(8,128)(2,1)}, u32[]{:S(2)}, u32[]{:S(2)}) collective-permute-start(bf16[192,2048]{1,0:T(8,128)(2,1)S(1)} %copy-done.41), channel_id=1, source_target_pairs={{0,3},{1,2},{2,1},{3,0},{4,7},{5,6},{6,5},{7,4},{8,11},{9,10},{10,... | collective-permute-start | bytes 2359304 | tf_op jit(solution)/shard_map/ppermute | solution.py:60
  60.4 21.2 %collective-permute-start.14 = (bf16[5,128,768]{2,1,0:T(8,128)(2,1)}, bf16[5,128,768]{2,1,0:T(8,128)(2,1)}, u32[]{:S(2)}, u32[]{:S(2)}) collective-permute-start(bf16[5,128,768]{2,1,0:T(8,128)(2,1)} %pad_maximum_fusion.1), channel_id=1, source_target_pairs={{0,1},{1,0},{2,3},{3,2},{4,5},{5,4},{6,7},{7,6},{8,9},{9,8},{10,11... | collective-permute-start | bytes 2949128 | tf_op jit(solution)/shard_map/ppermute | solution.py:60
  60.7 28.4 %collective-permute-start.16 = (bf16[4,96,2048]{2,1,0:T(8,128)(2,1)S(1)}, bf16[4,96,2048]{2,1,0:T(8,128)(2,1)}, u32[]{:S(2)}, u32[]{:S(2)}) collective-permute-start(bf16[4,96,2048]{2,1,0:T(8,128)(2,1)S(1)} %all-to-all-done.refs_0_.refs_4_), channel_id=1, source_target_pairs={{0,16},{1,17},{2,18},{3,19},{4,20},{5,21},{6,22},{7,23},{8,24},{9,... | collective-permute-start | bytes 4718600 | tf_op jit(solution)/shard_map/ppermute | solution.py:585
  65.2 21.2 %collective-permute-start.12 = (bf16[2,256,768]{2,1,0:T(8,128)(2,1)}, bf16[2,256,768]{2,1,0:T(8,128)(2,1)}, u32[]{:S(2)}, u32[]{:S(2)}) collective-permute-start(bf16[2,256,768]{2,1,0:T(8,128)(2,1)} %copy-done.36), channel_id=1, source_target_pairs={{0,4},{1,5},{2,6},{3,7},{4,8},{5,9},{6,10},{7,11},{8,12},{9,13},{1... | collective-permute-start | bytes 2359304 | tf_op jit(solution)/shard_map/ppermute | solution.py:60
  65.5 20.9 %collective-permute-start.13 = (bf16[2,256,768]{2,1,0:T(8,128)(2,1)S(1)}, bf16[2,256,768]{2,1,0:T(8,128)(2,1)}, u32[]{:S(2)}, u32[]{:S(2)}) collective-permute-start(bf16[2,256,768]{2,1,0:T(8,128)(2,1)S(1)} %maximum_select_fusion.refs_4_.refs_0_), channel_id=1, source_target_pairs={{0,12},{1,13},{2,14},{3,15},{4,0},{5,1},{6,2},{7,3},{8,4},{9,5},{1... | collective-permute-start | bytes 2359304 | tf_op jit(solution)/shard_map/ppermute | solution.py:60
  68.4 20.6 %collective-permute-start.15 = (bf16[192,2048]{1,0:T(8,128)(2,1)}, bf16[192,2048]{1,0:T(8,128)(2,1)}, u32[]{:S(2)}, u32[]{:S(2)}) collective-permute-start(bf16[192,2048]{1,0:T(8,128)(2,1)} %copy-done.39), channel_id=1, source_target_pairs={{0,3},{1,2},{2,1},{3,0},{4,7},{5,6},{6,5},{7,4},{8,11},{9,10},{10,... | collective-permute-start | bytes 2359304 | tf_op jit(solution)/shard_map/ppermute | solution.py:60
  89.1 25.7 %all-to-all-start.2 = ((bf16[4,48,2048]{2,1,0:T(8,128)(2,1)}), bf16[4,48,2048]{2,1,0:T(8,128)(2,1)}, u32[]{:S(2)}, u32[]{:S(2)}) async-start(bf16[4,48,2048]{2,1,0:T(8,128)(2,1)} %bitcast.8), calls=%async_computation.2 | async-start | bytes 1572864 | tf_op jit(solution)/shard_map/all_to_all | solution.py:63
  93.6 21.2 %collective-permute-start.20 = (bf16[3,128,768]{2,1,0:T(8,128)(2,1)}, bf16[3,128,768]{2,1,0:T(8,128)(2,1)}, u32[]{:S(2)}, u32[]{:S(2)}) collective-permute-start(bf16[3,128,768]{2,1,0:T(8,128)(2,1)} %get-tuple-element.128), channel_id=1, source_target_pairs={{0,1},{1,0},{2,3},{3,2},{4,5},{5,4},{6,7},{7,6},{8,9},{9,8},{10,11... | collective-permute-start | bytes 1769480 | tf_op jit(solution)/shard_map/ppermute | solution.py:60
  94.4 19.7 %collective-permute-start.19 = (bf16[1,256,768]{2,1,0:T(8,128)(2,1)}, bf16[1,256,768]{2,1,0:T(8,128)(2,1)S(1)}, u32[]{:S(2)}, u32[]{:S(2)}) collective-permute-start(bf16[1,256,768]{2,1,0:T(8,128)(2,1)} %maximum_select_fusion.1.refs_14_.refs_16_), channel_id=1, source_target_pairs={{0,12},{1,13},{2,14},{3,15},{4,0},{5,1},{6,2},{7,3},{8,4},{9,5},{1... | collective-permute-start | bytes 1179656 | tf_op jit(solution)/shard_map/ppermute | solution.py:60
  132.2 24.7 %collective-permute-start.26 = (bf16[4,128,768]{2,1,0:T(8,128)(2,1)S(1)}, bf16[4,128,768]{2,1,0:T(8,128)(2,1)S(1)}, u32[]{:S(2)}, u32[]{:S(2)}) collective-permute-start(bf16[4,128,768]{2,1,0:T(8,128)(2,1)S(1)} %get-tuple-element.149), channel_id=1, source_target_pairs={{0,1},{1,0},{2,3},{3,2},{4,5},{5,4},{6,7},{7,6},{8,9},{9,8},{10,11... | collective-permute-start | bytes 2359304 | tf_op jit(solution)/shard_map/ppermute | solution.py:60
  133.4 23.4 %collective-permute-start.25 = (bf16[1,256,768]{2,1,0:T(8,128)(2,1)S(1)}, bf16[1,256,768]{2,1,0:T(8,128)(2,1)S(1)}, u32[]{:S(2)}, u32[]{:S(2)}) collective-permute-start(bf16[1,256,768]{2,1,0:T(8,128)(2,1)S(1)} %get-tuple-element.148), channel_id=1, source_target_pairs={{0,4},{1,5},{2,6},{3,7},{4,8},{5,9},{6,10},{7,11},{8,12},{9,13},{1... | collective-permute-start | bytes 1179656 | tf_op jit(solution)/shard_map/ppermute | solution.py:60
  133.4 23.5 %collective-permute-start.24 = (bf16[1,256,768]{2,1,0:T(8,128)(2,1)S(1)}, bf16[1,256,768]{2,1,0:T(8,128)(2,1)S(1)}, u32[]{:S(2)}, u32[]{:S(2)}) collective-permute-start(bf16[1,256,768]{2,1,0:T(8,128)(2,1)S(1)} %get-tuple-element.146), channel_id=1, source_target_pairs={{0,12},{1,13},{2,14},{3,15},{4,0},{5,1},{6,2},{7,3},{8,4},{9,5},{1... | collective-permute-start | bytes 1179656 | tf_op jit(solution)/shard_map/ppermute | solution.py:60
  156.9 23.1 %collective-permute-start.27 = (bf16[2,256,768]{2,1,0:T(8,128)(2,1)S(1)}, bf16[2,256,768]{2,1,0:T(8,128)(2,1)S(1)}, u32[]{:S(2)}, u32[]{:S(2)}) collective-permute-start(bf16[2,256,768]{2,1,0:T(8,128)(2,1)S(1)} %get-tuple-element.151), channel_id=1, source_target_pairs={{0,12},{1,13},{2,14},{3,15},{4,0},{5,1},{6,2},{7,3},{8,4},{9,5},{1... | collective-permute-start | bytes 2359304 | tf_op jit(solution)/shard_map/ppermute | solution.py:60
  159.0 21.0 %collective-permute-start.28 = (bf16[2,256,768]{2,1,0:T(8,128)(2,1)S(1)}, bf16[2,256,768]{2,1,0:T(8,128)(2,1)S(1)}, u32[]{:S(2)}, u32[]{:S(2)}) collective-permute-start(bf16[2,256,768]{2,1,0:T(8,128)(2,1)S(1)} %get-tuple-element.153), channel_id=1, source_target_pairs={{0,4},{1,5},{2,6},{3,7},{4,8},{5,9},{6,10},{7,11},{8,12},{9,13},{1... | collective-permute-start | bytes 2359304 | tf_op jit(solution)/shard_map/ppermute | solution.py:60
  159.0 21.0 %collective-permute-start.29 = (bf16[2,2,128,768]{3,2,1,0:T(8,128)(2,1)S(1)}, bf16[2,2,128,768]{3,2,1,0:T(8,128)(2,1)S(1)}, u32[]{:S(2)}, u32[]{:S(2)}) collective-permute-start(bf16[2,2,128,768]{3,2,1,0:T(8,128)(2,1)S(1)} %get-tuple-element.154), channel_id=1, source_target_pairs={{0,1},{1,0},{2,3},{3,2},{4,5},{5,4},{6,7},{7,6},{8,9},{9,8},{10,11... | collective-permute-start | bytes 2359304 | tf_op jit(solution)/shard_map/ppermute | solution.py:60
  160.7 19.3 %collective-permute-start.30 = (bf16[1,128,768]{2,1,0:T(8,128)(2,1)S(1)}, bf16[1,128,768]{2,1,0:T(8,128)(2,1)S(1)}, u32[]{:S(2)}, u32[]{:S(2)}) collective-permute-start(bf16[1,128,768]{2,1,0:T(8,128)(2,1)S(1)} %get-tuple-element.156), channel_id=1, source_target_pairs={{0,12},{1,13},{2,14},{3,15},{4,0},{5,1},{6,2},{7,3},{8,4},{9,5},{1... | collective-permute-start | bytes 589832 | tf_op jit(solution)/shard_map/ppermute | solution.py:60
  183.2 29.1 %collective-permute-start.31 = (bf16[2,256,768]{2,1,0:T(8,128)(2,1)}, bf16[2,256,768]{2,1,0:T(8,128)(2,1)}, u32[]{:S(2)}, u32[]{:S(2)}) collective-permute-start(bf16[2,256,768]{2,1,0:T(8,128)(2,1)} %get-tuple-element.165), channel_id=1, source_target_pairs={{0,4},{1,5},{2,6},{3,7},{4,8},{5,9},{6,10},{7,11},{8,12},{9,13},{1... | collective-permute-start | bytes 2359304 | tf_op jit(solution)/shard_map/ppermute | solution.py:60
  183.2 29.1 %collective-permute-start.32 = (bf16[2,2,128,768]{3,2,1,0:T(8,128)(2,1)}, bf16[2,2,128,768]{3,2,1,0:T(8,128)(2,1)}, u32[]{:S(2)}, u32[]{:S(2)}) collective-permute-start(bf16[2,2,128,768]{3,2,1,0:T(8,128)(2,1)} %get-tuple-element.167), channel_id=1, source_target_pairs={{0,1},{1,0},{2,3},{3,2},{4,5},{5,4},{6,7},{7,6},{8,9},{9,8},{10,11... | collective-permute-start | bytes 2359304 | tf_op jit(solution)/shard_map/ppermute | solution.py:60
  184.0 28.3 %collective-permute-start.33 = (bf16[5,128,768]{2,1,0:T(8,128)(2,1)}, bf16[5,128,768]{2,1,0:T(8,128)(2,1)}, u32[]{:S(2)}, u32[]{:S(2)}) collective-permute-start(bf16[5,128,768]{2,1,0:T(8,128)(2,1)} %get-tuple-element.169), channel_id=1, source_target_pairs={{0,12},{1,13},{2,14},{3,15},{4,0},{5,1},{6,2},{7,3},{8,4},{9,5},{1... | collective-permute-start | bytes 2949128 | tf_op jit(solution)/shard_map/ppermute | solution.py:60
  215.2 19.5 %collective-permute-start.38 = (bf16[192,2048]{1,0:T(8,128)(2,1)}, bf16[192,2048]{1,0:T(8,128)(2,1)}, u32[]{:S(2)}, u32[]{:S(2)}) collective-permute-start(bf16[192,2048]{1,0:T(8,128)(2,1)} %bitcast.15), channel_id=1, source_target_pairs={{0,3},{1,2},{2,1},{3,0},{4,7},{5,6},{6,5},{7,4},{8,11},{9,10},{10,... | collective-permute-start | bytes 2359304 | tf_op jit(solution)/shard_map/ppermute | solution.py:60
  244.2 31.5 %collective-permute-start.41 = (bf16[192,2048]{1,0:T(8,128)(2,1)}, bf16[192,2048]{1,0:T(8,128)(2,1)S(1)}, u32[]{:S(2)}, u32[]{:S(2)}) collective-permute-start(bf16[192,2048]{1,0:T(8,128)(2,1)} %bitcast.19), channel_id=1, source_target_pairs={{0,3},{1,2},{2,1},{3,0},{4,7},{5,6},{6,5},{7,4},{8,11},{9,10},{10,... | collective-permute-start | bytes 2359304 | tf_op jit(solution)/shard_map/ppermute | solution.py:60
  (82 other events, 808.0 us)

commit v3 on v2

--- a/solution.py
+++ b/solution.py
@@ -693,7 +693,11 @@
     stay = jnp.where(low == 0, low_half, high_half)
     leave_got = send("side", jnp.where(low == 0, high_half, low_half))
     out_oth = send("mirror", out_home.reshape(quarter, depth))
-    out_own = r.exchange(r.late(out[:quarter]).reshape(4, MOST, depth), 2)
+    own_rows = r.hold(
+        jnp.concatenate(
+            [r.late(v[:quarter]).reshape(4, MOST, depth) for v in (out, grd)], axis=1
+        )
+    )
     r.next()
     here = core == side
     mir_back = r.pin(mir_back)
@@ -701,8 +705,9 @@
     gu_mir = add(mir_keep[0], got_b[0], mir_back[:2], r.pin(mir_near))
     away = send("mirror", join(gu_mir, mine[2:]))
     grad_oth = send("mirror", grad_home.reshape(quarter, depth))
-    grad_own = r.exchange(r.late(grd[:quarter]).reshape(4, MOST, depth))
-    out_own, grad_own = out_own.reshape(quarter, depth), grad_own.reshape(quarter, depth)
+    owned = r.exchange(own_rows)
+    out_own = owned[:, :MOST].reshape(quarter, depth)
+    grad_own = owned[:, MOST:].reshape(quarter, depth)
     own = join(mine[:2], add(own_sum[:1], mir_back[2:], own_near))
     other = lax.ppermute(jnp.where(here, away, own), AXES, TO_CORE)
     kept = jnp.where(here, own, away)

time: 283 us -> 276 us (0.975)
  waiting for transfers between devices: 81 us -> 76.1 us
  starting transfers between devices: 81.7 us -> 77.5 us
    all_to_all x7 -> x6, waiting for transfers between devices: 28.4 us -> 17.3 us  [exchange(): lax.all_to_all(value, 'expert', split_axis=0, concat_axis=0, tiled=True,...]
    ppermute x38, waiting for transfers between devices: 52.6 us -> 58.3 us  [send(): return self.hold(lax.ppermute(value, AXES, MOVES[link]), rounds)]
    all_to_all x7 -> x6, starting transfers between devices: 32.5 us -> 28.2 us  [exchange(): lax.all_to_all(value, 'expert', split_axis=0, concat_axis=0, tiled=True,...]
    unnamed x112 -> x114, local copies, waits for them, and re-layouts: 17.4 us -> 16.2 us
  transfers between devices with their start and end apart: 49 -> 48, of which waited for: 19 -> 19; matrix products, arithmetic and copies ran while one was open for 9% -> 12% of each run, Pallas kernels for 23% -> 24%
where the time goes in v3:
time: 276 us; the launch traced here: 274 us
  starting transfers between devices  77.5 us (28%)
  waiting for transfers between devices  76.1 us (28%)
  Pallas kernels  70.8 us (26%)
  local copies, waits for them, and re-layouts  26.5 us (10%)
  other arithmetic  21.5 us (8%)
    pallas_call x8, Pallas kernels, run(): pl.pallas_call(kernel, out_shape=shapes, in_specs=[pl.BlockSpec(memory_sp...  63.7 us
    ppermute x38, waiting for transfers between devices, send(): return self.hold(lax.ppermute(value, AXES, MOVES[link]), rounds)  58.3 us
    ppermute x38, starting transfers between devices, send(): return self.hold(lax.ppermute(value, AXES, MOVES[link]), rounds)  49.2 us
    all_to_all x6, starting transfers between devices, exchange(): lax.all_to_all(value, 'expert', split_axis=0, concat_axis=0, tiled=True,...  28.2 us
    all_to_all x6, waiting for transfers between devices, exchange(): lax.all_to_all(value, 'expert', split_axis=0, concat_axis=0, tiled=True,...  17.3 us
    unnamed x114, local copies, waits for them, and re-layouts  16.2 us
    convert_element_type x9, other arithmetic, add(): return sum((t.astype(F32) for t in terms)).astype(BF16)  10.2 us
  transfers between devices with their start and end apart: 48, of which 19 were waited for; matrix products, arithmetic and copies ran while one was open for 12% of the time, Pallas kernels for 24%

profile of v3, /device:TPU:0, one launch (start us, length us, event | category | flops | bytes accessed | tf_op | source)
XLA Modules:
  0.0 273.6 jit_solution(12615879002696823659)
XLA Ops:
  14.4 3.9 %collective-permute-done.4.refs_9_.refs_11_ = bf16[1,128,768]{2,1,0:T(8,128)(2,1)S(1)} collective-permute-done((bf16[1,128,768]{2,1,0:T(8,128)(2,1)S(1)}, bf16[1,128,768]{2,1,0:T(8,128)(2,1)S(1)}, u32[]{:S(2)}, u32[]{:S(2)}) %collective-permute-start.4) | collective-permute-done | bytes 196640 | tf_op jit(solution)/shard_map/ppermute | solution.py:60
  18.3 3.4 %collective-permute-done.3.refs_10_.refs_12_ = bf16[1,128,768]{2,1,0:T(8,128)(2,1)S(1)} collective-permute-done((bf16[1,128,768]{2,1,0:T(8,128)(2,1)S(1)}, bf16[1,128,768]{2,1,0:T(8,128)(2,1)S(1)}, u32[]{:S(2)}, u32[]{:S(2)}) %collective-permute-start.3) | collective-permute-done | bytes 196640 | tf_op jit(solution)/shard_map/ppermute | solution.py:60
  31.1 5.3 %all-to-all-start = ((bf16[4,96,2048]{2,1,0:T(8,128)(2,1)}), bf16[4,96,2048]{2,1,0:T(8,128)(2,1)S(1)}, u32[]{:S(2)}, u32[]{:S(2)}) async-start(bf16[4,96,2048]{2,1,0:T(8,128)(2,1)} %bitcast.6), calls=%async_computation | async-start | bytes 3145728 | tf_op jit(solution)/shard_map/all_to_all | solution.py:63
  44.0 10.3 %collective-permute-done.10.refs_11_.refs_7_.refs_13_ = bf16[3,128,768]{2,1,0:T(8,128)(2,1)S(1)} collective-permute-done((bf16[3,128,768]{2,1,0:T(8,128)(2,1)S(1)}, bf16[3,128,768]{2,1,0:T(8,128)(2,1)S(1)}, u32[]{:S(2)}, u32[]{:S(2)}) %collective-permute-start.10) | collective-permute-done | bytes 589856 | tf_op jit(solution)/shard_map/ppermute | solution.py:60
  60.7 4.5 %all-to-all-start.1 = ((bf16[4,48,2048]{2,1,0:T(8,128)(2,1)}), bf16[4,48,2048]{2,1,0:T(8,128)(2,1)S(1)}, u32[]{:S(2)}, u32[]{:S(2)}) async-start(bf16[4,48,2048]{2,1,0:T(8,128)(2,1)} %bitcast.7), calls=%async_computation.1 | async-start | bytes 1572864 | tf_op jit(solution)/shard_map/all_to_all | solution.py:63
  69.6 8.6 %all-to-all-done.1.refs_1_.refs_5_ = bf16[4,48,2048]{2,1,0:T(8,128)(2,1)S(1)} async-done(((bf16[4,48,2048]{2,1,0:T(8,128)(2,1)}), bf16[4,48,2048]{2,1,0:T(8,128)(2,1)S(1)}, u32[]{:S(2)}, u32[]{:S(2)}) %all-to-all-start.1) | async-done | bytes 786464 | tf_op jit(solution)/shard_map/all_to_all | solution.py:63
  78.2 3.4 %collective-permute-done.14.refs_13_.refs_9_.refs_15_ = bf16[5,128,768]{2,1,0:T(8,128)(2,1)} collective-permute-done((bf16[5,128,768]{2,1,0:T(8,128)(2,1)}, bf16[5,128,768]{2,1,0:T(8,128)(2,1)}, u32[]{:S(2)}, u32[]{:S(2)}) %collective-permute-start.14) | collective-permute-done | bytes 983072 | tf_op jit(solution)/shard_map/ppermute | solution.py:60
  89.1 4.5 %all-to-all-start.2 = ((bf16[4,48,2048]{2,1,0:T(8,128)(2,1)}), bf16[4,48,2048]{2,1,0:T(8,128)(2,1)}, u32[]{:S(2)}, u32[]{:S(2)}) async-start(bf16[4,48,2048]{2,1,0:T(8,128)(2,1)} %bitcast.8), calls=%async_computation.2 | async-start | bytes 1572864 | tf_op jit(solution)/shard_map/all_to_all | solution.py:63
  100.6 12.4 %forward.1 = (bf16[768,768]{1,0:T(8,128)(2,1)S(1)}, f32[768,768]{1,0:T(8,128)}, f32[768,768]{1,0:T(8,128)}) custom-call(s32[4]{0:T(128)S(1)} %pad_add_fusion.place, bf16[4,96,2048]{2,1,0:T(8,128)(2,1)} %copy-done.1, bf16[4,48,2048]{2,1,0:T(8,128)(2,1)S(1)} %all-to-all-done.1.refs_1_.refs_5_, bf16[4,96,2048]{2,1,0:T(8,128)(2,1)} %collective-permute-done.16.refs_2_.refs_6_, ...), custom_call_target="tpu_custom_call" | custom-call | flops 4831838208 | bytes 17498112 | tf_op jit(solution)/shard_map/forward/pallas_call | solution.py:502
  116.9 3.2 %collective-permute-start.22 = (bf16[1,128,768]{2,1,0:T(8,128)(2,1)S(1)}, bf16[1,128,768]{2,1,0:T(8,128)(2,1)S(1)}, u32[]{:S(2)}, u32[]{:S(2)}) collective-permute-start(bf16[1,128,768]{2,1,0:T(8,128)(2,1)S(1)} %slice.95), channel_id=1, source_target_pairs={{0,12},{1,13},{2,14},{3,15},{4,0},{5,1},{6,2},{7,3},{8,4},{9,5},{1... | collective-permute-start | bytes 589832 | tf_op jit(solution)/shard_map/ppermute | solution.py:60
  121.4 10.0 %down_term.1 = (bf16[4,128,768]{2,1,0:T(8,128)(2,1)S(1)}, bf16[4,128,768]{2,1,0:T(8,128)(2,1)S(1)}, bf16[1,256,768]{2,1,0:T(8,128)(2,1)S(1)}, bf16[1,256,768]{2,...) custom-call(s32[4]{0:T(128)S(1)} %pad_add_fusion.place, ...), custom_call_target="tpu_custom_call" | custom-call | flops 2415919104 | bytes 9043968 | tf_op jit(solution)/shard_map/down_term/pallas_call | solution.py:502
  133.4 3.2 %collective-permute-start.24 = (bf16[1,256,768]{2,1,0:T(8,128)(2,1)S(1)}, bf16[1,256,768]{2,1,0:T(8,128)(2,1)S(1)}, u32[]{:S(2)}, u32[]{:S(2)}) collective-permute-start(bf16[1,256,768]{2,1,0:T(8,128)(2,1)S(1)} %get-tuple-element.146), channel_id=1, source_target_pairs={{0,12},{1,13},{2,14},{3,15},{4,0},{5,1},{6,2},{7,3},{8,4},{9,5},{1... | collective-permute-start | bytes 1179656 | tf_op jit(solution)/shard_map/ppermute | solution.py:60
  136.7 20.1 %gradient.1 = (bf16[2,768,768]{2,1,0:T(8,128)(2,1)}, bf16[2,256,768]{2,1,0:T(8,128)(2,1)S(1)}, bf16[2,256,768]{2,1,0:T(8,128)(2,1)S(1)}, bf16[2,256,768]{2,1,0:T...) custom-call(s32[4]{0:T(128)S(1)} %pad_add_fusion.place, ...), custom_call_target="tpu_custom_call" | custom-call | flops 7247757312 | bytes 27131904 | tf_op jit(solution)/shard_map/gradient/pallas_call | solution.py:502
  160.7 3.2 %collective-permute-start.30 = (bf16[1,128,768]{2,1,0:T(8,128)(2,1)S(1)}, bf16[1,128,768]{2,1,0:T(8,128)(2,1)S(1)}, u32[]{:S(2)}, u32[]{:S(2)}) collective-permute-start(bf16[1,128,768]{2,1,0:T(8,128)(2,1)S(1)} %get-tuple-element.156), channel_id=1, source_target_pairs={{0,12},{1,13},{2,14},{3,15},{4,0},{5,1},{6,2},{7,3},{8,4},{9,5},{1... | collective-permute-start | bytes 589832 | tf_op jit(solution)/shard_map/ppermute | solution.py:60
  163.9 15.2 %outputs.1 = (f32[384,2048]{1,0:T(8,128)}, f32[384,2048]{1,0:T(8,128)}, bf16[768,2048]{1,0:T(8,128)(2,1)}) custom-call(s32[4]{0:T(128)S(1)} %pad_add_fusion.place, bf16[768,768]{1,0:T(8,128)(2,1)} %copy-done.44, bf16[2,768,768]{2,1,0:T(8,128)(2,1)} %get-tuple-element.158.both_ref, bf16[2,256,768]{2,1,0:T(8,128)(2,1)S(1)} %maximum_select_fusion.refs_4_.refs_0_, ...), custom_call_target="tpu_custom_call" | custom-call | flops 7247757312 | bytes 24182784 | tf_op jit(solution)/shard_map/outputs/pallas_call | solution.py:502
  184.0 3.2 %collective-permute-start.33 = (bf16[5,128,768]{2,1,0:T(8,128)(2,1)}, bf16[5,128,768]{2,1,0:T(8,128)(2,1)}, u32[]{:S(2)}, u32[]{:S(2)}) collective-permute-start(bf16[5,128,768]{2,1,0:T(8,128)(2,1)} %get-tuple-element.169), channel_id=1, source_target_pairs={{0,12},{1,13},{2,14},{3,15},{4,0},{5,1},{6,2},{7,3},{8,4},{9,5},{1... | collective-permute-start | bytes 2949128 | tf_op jit(solution)/shard_map/ppermute | solution.py:60
  190.9 4.9 %all-to-all-start.3 = ((bf16[4,48,2048]{2,1,0:T(8,128)(2,1)}), bf16[4,48,2048]{2,1,0:T(8,128)(2,1)}, u32[]{:S(2)}, u32[]{:S(2)}) async-start(bf16[4,48,2048]{2,1,0:T(8,128)(2,1)} %bitcast.9), calls=%async_computation.3 | async-start | bytes 1572864 | tf_op jit(solution)/shard_map/all_to_all | solution.py:63
  199.4 8.7 %all-to-all-done.3 = bf16[4,48,2048]{2,1,0:T(8,128)(2,1)} async-done(((bf16[4,48,2048]{2,1,0:T(8,128)(2,1)}), bf16[4,48,2048]{2,1,0:T(8,128)(2,1)}, u32[]{:S(2)}, u32[]{:S(2)}) %all-to-all-start.3) | async-done | bytes 786464 | tf_op jit(solution)/shard_map/all_to_all | solution.py:63
  208.1 4.2 %all-to-all-start.4 = ((bf16[4,48,2048]{2,1,0:T(8,128)(2,1)}), bf16[4,48,2048]{2,1,0:T(8,128)(2,1)}, u32[]{:S(2)}, u32[]{:S(2)}) async-start(bf16[4,48,2048]{2,1,0:T(8,128)(2,1)} %bitcast.42), calls=%async_computation.4 | async-start | bytes 1572864 | tf_op jit(solution)/shard_map/all_to_all | solution.py:63
  220.1 3.2 %collective-permute-start.37 = (bf16[2,128,768]{2,1,0:T(8,128)(2,1)}, bf16[2,128,768]{2,1,0:T(8,128)(2,1)}, u32[]{:S(2)}, u32[]{:S(2)}) collective-permute-start(bf16[2,128,768]{2,1,0:T(8,128)(2,1)} %fusion), channel_id=1, source_target_pairs={{0,12},{1,13},{2,14},{3,15},{4,0},{5,1},{6,2},{7,3},{8,4},{9,5},{1... | collective-permute-start | bytes 1179656 | tf_op jit(solution)/shard_map/ppermute | solution.py:60
  224.6 4.7 %all-to-all-start.5 = ((bf16[4,96,2048]{2,1,0:T(8,128)(2,1)}), bf16[4,96,2048]{2,1,0:T(8,128)(2,1)}, u32[]{:S(2)}, u32[]{:S(2)}) async-start(bf16[4,96,2048]{2,1,0:T(8,128)(2,1)} %pad_maximum_fusion), calls=%async_computation.5 | async-start | bytes 3145728 | tf_op jit(solution)/shard_map/all_to_all | solution.py:63
  242.7 13.3 %collective-permute-done.39 = bf16[3,128,768]{2,1,0:T(8,128)(2,1)} collective-permute-done((bf16[3,128,768]{2,1,0:T(8,128)(2,1)}, bf16[3,128,768]{2,1,0:T(8,128)(2,1)}, u32[]{:S(2)}, u32[]{:S(2)}) %collective-permute-start.39) | collective-permute-done | bytes 589856 | tf_op jit(solution)/shard_map/ppermute | solution.py:60
  262.3 7.0 %collective-permute-done.41.goth_ref = bf16[192,2048]{1,0:T(8,128)(2,1)S(1)} collective-permute-done((bf16[192,2048]{1,0:T(8,128)(2,1)}, bf16[192,2048]{1,0:T(8,128)(2,1)S(1)}, u32[]{:S(2)}, u32[]{:S(2)}) %collective-permute-start.41) | collective-permute-done | bytes 786464 | tf_op jit(solution)/shard_map/ppermute | solution.py:60
  269.3 4.4 %combine.1 = (bf16[256,2048]{1,0:T(8,128)(2,1)}, bf16[256,2048]{1,0:T(8,128)(2,1)}, f32[6,256]{1,0:T(8,128)}) custom-call(s32[4]{0:T(128)S(1)} %pad_add_fusion.place, s32[6,256]{1,0:T(8,128)S(1)} %bitcast.39, bf16[6,256]{1,0:T(8,128)(2,1)S(1)} %bitcast.41, bf16[256,2048]{1,0:T(8,128)(2,1)S(1)} %copy-done.35, bf16[192,2048]{1,0:T(8,128)(2,1)S(1)} %bitcast.37, ...), custom_call_target="tpu_custom_call" | custom-call | flops 2000000000 | bytes 8000000 | tf_op jit(solution)/shard_map/combine/pallas_call | solution.py:209
  (228 shorter events, 107.3 us)
Async XLA Ops:
  31.1 27.3 %all-to-all-start = ((bf16[4,96,2048]{2,1,0:T(8,128)(2,1)}), bf16[4,96,2048]{2,1,0:T(8,128)(2,1)S(1)}, u32[]{:S(2)}, u32[]{:S(2)}) async-start(bf16[4,96,2048]{2,1,0:T(8,128)(2,1)} %bitcast.6), calls=%async_computation | async-start | bytes 3145728 | tf_op jit(solution)/shard_map/all_to_all | solution.py:63
  38.3 22.1 %collective-permute-start.8 = (bf16[5,128,768]{2,1,0:T(8,128)(2,1)}, bf16[5,128,768]{2,1,0:T(8,128)(2,1)}, u32[]{:S(2)}, u32[]{:S(2)}) collective-permute-start(bf16[5,128,768]{2,1,0:T(8,128)(2,1)} %pad_maximum_fusion.1), channel_id=1, source_target_pairs={{0,1},{1,0},{2,3},{3,2},{4,5},{5,4},{6,7},{7,6},{8,9},{9,8},{10,11... | collective-permute-start | bytes 2949128 | tf_op jit(solution)/shard_map/ppermute | solution.py:60
  39.2 19.2 %collective-permute-start.11 = (bf16[192,2048]{1,0:T(8,128)(2,1)S(1)}, bf16[192,2048]{1,0:T(8,128)(2,1)}, u32[]{:S(2)}, u32[]{:S(2)}) collective-permute-start(bf16[192,2048]{1,0:T(8,128)(2,1)S(1)} %copy-done.41), channel_id=1, source_target_pairs={{0,3},{1,2},{2,1},{3,0},{4,7},{5,6},{6,5},{7,4},{8,11},{9,10},{10,... | collective-permute-start | bytes 2359304 | tf_op jit(solution)/shard_map/ppermute | solution.py:60
  60.4 21.2 %collective-permute-start.14 = (bf16[5,128,768]{2,1,0:T(8,128)(2,1)}, bf16[5,128,768]{2,1,0:T(8,128)(2,1)}, u32[]{:S(2)}, u32[]{:S(2)}) collective-permute-start(bf16[5,128,768]{2,1,0:T(8,128)(2,1)} %pad_maximum_fusion.2), channel_id=1, source_target_pairs={{0,1},{1,0},{2,3},{3,2},{4,5},{5,4},{6,7},{7,6},{8,9},{9,8},{10,11... | collective-permute-start | bytes 2949128 | tf_op jit(solution)/shard_map/ppermute | solution.py:60
  60.7 28.4 %collective-permute-start.16 = (bf16[4,96,2048]{2,1,0:T(8,128)(2,1)S(1)}, bf16[4,96,2048]{2,1,0:T(8,128)(2,1)}, u32[]{:S(2)}, u32[]{:S(2)}) collective-permute-start(bf16[4,96,2048]{2,1,0:T(8,128)(2,1)S(1)} %all-to-all-done.refs_0_.refs_4_), channel_id=1, source_target_pairs={{0,16},{1,17},{2,18},{3,19},{4,20},{5,21},{6,22},{7,23},{8,24},{9,... | collective-permute-start | bytes 4718600 | tf_op jit(solution)/shard_map/ppermute | solution.py:585
  65.2 21.2 %collective-permute-start.12 = (bf16[2,256,768]{2,1,0:T(8,128)(2,1)}, bf16[2,256,768]{2,1,0:T(8,128)(2,1)}, u32[]{:S(2)}, u32[]{:S(2)}) collective-permute-start(bf16[2,256,768]{2,1,0:T(8,128)(2,1)} %copy-done.36), channel_id=1, source_target_pairs={{0,4},{1,5},{2,6},{3,7},{4,8},{5,9},{6,10},{7,11},{8,12},{9,13},{1... | collective-permute-start | bytes 2359304 | tf_op jit(solution)/shard_map/ppermute | solution.py:60
  65.5 20.9 %collective-permute-start.13 = (bf16[2,256,768]{2,1,0:T(8,128)(2,1)S(1)}, bf16[2,256,768]{2,1,0:T(8,128)(2,1)}, u32[]{:S(2)}, u32[]{:S(2)}) collective-permute-start(bf16[2,256,768]{2,1,0:T(8,128)(2,1)S(1)} %maximum_select_fusion.refs_4_.refs_0_), channel_id=1, source_target_pairs={{0,12},{1,13},{2,14},{3,15},{4,0},{5,1},{6,2},{7,3},{8,4},{9,5},{1... | collective-permute-start | bytes 2359304 | tf_op jit(solution)/shard_map/ppermute | solution.py:60
  68.4 20.6 %collective-permute-start.15 = (bf16[192,2048]{1,0:T(8,128)(2,1)}, bf16[192,2048]{1,0:T(8,128)(2,1)}, u32[]{:S(2)}, u32[]{:S(2)}) collective-permute-start(bf16[192,2048]{1,0:T(8,128)(2,1)} %copy-done.39), channel_id=1, source_target_pairs={{0,3},{1,2},{2,1},{3,0},{4,7},{5,6},{6,5},{7,4},{8,11},{9,10},{10,... | collective-permute-start | bytes 2359304 | tf_op jit(solution)/shard_map/ppermute | solution.py:60
  89.1 25.8 %all-to-all-start.2 = ((bf16[4,48,2048]{2,1,0:T(8,128)(2,1)}), bf16[4,48,2048]{2,1,0:T(8,128)(2,1)}, u32[]{:S(2)}, u32[]{:S(2)}) async-start(bf16[4,48,2048]{2,1,0:T(8,128)(2,1)} %bitcast.8), calls=%async_computation.2 | async-start | bytes 1572864 | tf_op jit(solution)/shard_map/all_to_all | solution.py:63
  93.6 21.2 %collective-permute-start.20 = (bf16[3,128,768]{2,1,0:T(8,128)(2,1)}, bf16[3,128,768]{2,1,0:T(8,128)(2,1)}, u32[]{:S(2)}, u32[]{:S(2)}) collective-permute-start(bf16[3,128,768]{2,1,0:T(8,128)(2,1)} %get-tuple-element.128), channel_id=1, source_target_pairs={{0,1},{1,0},{2,3},{3,2},{4,5},{5,4},{6,7},{7,6},{8,9},{9,8},{10,11... | collective-permute-start | bytes 1769480 | tf_op jit(solution)/shard_map/ppermute | solution.py:60
  94.4 19.7 %collective-permute-start.19 = (bf16[1,256,768]{2,1,0:T(8,128)(2,1)}, bf16[1,256,768]{2,1,0:T(8,128)(2,1)S(1)}, u32[]{:S(2)}, u32[]{:S(2)}) collective-permute-start(bf16[1,256,768]{2,1,0:T(8,128)(2,1)} %maximum_select_fusion.1.refs_14_.refs_16_), channel_id=1, source_target_pairs={{0,12},{1,13},{2,14},{3,15},{4,0},{5,1},{6,2},{7,3},{8,4},{9,5},{1... | collective-permute-start | bytes 1179656 | tf_op jit(solution)/shard_map/ppermute | solution.py:60
  132.2 24.7 %collective-permute-start.26 = (bf16[4,128,768]{2,1,0:T(8,128)(2,1)S(1)}, bf16[4,128,768]{2,1,0:T(8,128)(2,1)S(1)}, u32[]{:S(2)}, u32[]{:S(2)}) collective-permute-start(bf16[4,128,768]{2,1,0:T(8,128)(2,1)S(1)} %get-tuple-element.149), channel_id=1, source_target_pairs={{0,1},{1,0},{2,3},{3,2},{4,5},{5,4},{6,7},{7,6},{8,9},{9,8},{10,11... | collective-permute-start | bytes 2359304 | tf_op jit(solution)/shard_map/ppermute | solution.py:60
  133.4 23.4 %collective-permute-start.25 = (bf16[1,256,768]{2,1,0:T(8,128)(2,1)S(1)}, bf16[1,256,768]{2,1,0:T(8,128)(2,1)S(1)}, u32[]{:S(2)}, u32[]{:S(2)}) collective-permute-start(bf16[1,256,768]{2,1,0:T(8,128)(2,1)S(1)} %get-tuple-element.148), channel_id=1, source_target_pairs={{0,4},{1,5},{2,6},{3,7},{4,8},{5,9},{6,10},{7,11},{8,12},{9,13},{1... | collective-permute-start | bytes 1179656 | tf_op jit(solution)/shard_map/ppermute | solution.py:60
  133.4 23.5 %collective-permute-start.24 = (bf16[1,256,768]{2,1,0:T(8,128)(2,1)S(1)}, bf16[1,256,768]{2,1,0:T(8,128)(2,1)S(1)}, u32[]{:S(2)}, u32[]{:S(2)}) collective-permute-start(bf16[1,256,768]{2,1,0:T(8,128)(2,1)S(1)} %get-tuple-element.146), channel_id=1, source_target_pairs={{0,12},{1,13},{2,14},{3,15},{4,0},{5,1},{6,2},{7,3},{8,4},{9,5},{1... | collective-permute-start | bytes 1179656 | tf_op jit(solution)/shard_map/ppermute | solution.py:60
  156.9 23.1 %collective-permute-start.27 = (bf16[2,256,768]{2,1,0:T(8,128)(2,1)S(1)}, bf16[2,256,768]{2,1,0:T(8,128)(2,1)S(1)}, u32[]{:S(2)}, u32[]{:S(2)}) collective-permute-start(bf16[2,256,768]{2,1,0:T(8,128)(2,1)S(1)} %get-tuple-element.151), channel_id=1, source_target_pairs={{0,12},{1,13},{2,14},{3,15},{4,0},{5,1},{6,2},{7,3},{8,4},{9,5},{1... | collective-permute-start | bytes 2359304 | tf_op jit(solution)/shard_map/ppermute | solution.py:60
  159.0 21.0 %collective-permute-start.28 = (bf16[2,256,768]{2,1,0:T(8,128)(2,1)S(1)}, bf16[2,256,768]{2,1,0:T(8,128)(2,1)S(1)}, u32[]{:S(2)}, u32[]{:S(2)}) collective-permute-start(bf16[2,256,768]{2,1,0:T(8,128)(2,1)S(1)} %get-tuple-element.153), channel_id=1, source_target_pairs={{0,4},{1,5},{2,6},{3,7},{4,8},{5,9},{6,10},{7,11},{8,12},{9,13},{1... | collective-permute-start | bytes 2359304 | tf_op jit(solution)/shard_map/ppermute | solution.py:60
  159.0 21.0 %collective-permute-start.29 = (bf16[2,2,128,768]{3,2,1,0:T(8,128)(2,1)S(1)}, bf16[2,2,128,768]{3,2,1,0:T(8,128)(2,1)S(1)}, u32[]{:S(2)}, u32[]{:S(2)}) collective-permute-start(bf16[2,2,128,768]{3,2,1,0:T(8,128)(2,1)S(1)} %get-tuple-element.154), channel_id=1, source_target_pairs={{0,1},{1,0},{2,3},{3,2},{4,5},{5,4},{6,7},{7,6},{8,9},{9,8},{10,11... | collective-permute-start | bytes 2359304 | tf_op jit(solution)/shard_map/ppermute | solution.py:60
  160.7 19.3 %collective-permute-start.30 = (bf16[1,128,768]{2,1,0:T(8,128)(2,1)S(1)}, bf16[1,128,768]{2,1,0:T(8,128)(2,1)S(1)}, u32[]{:S(2)}, u32[]{:S(2)}) collective-permute-start(bf16[1,128,768]{2,1,0:T(8,128)(2,1)S(1)} %get-tuple-element.156), channel_id=1, source_target_pairs={{0,12},{1,13},{2,14},{3,15},{4,0},{5,1},{6,2},{7,3},{8,4},{9,5},{1... | collective-permute-start | bytes 589832 | tf_op jit(solution)/shard_map/ppermute | solution.py:60
  183.2 29.1 %collective-permute-start.31 = (bf16[2,256,768]{2,1,0:T(8,128)(2,1)}, bf16[2,256,768]{2,1,0:T(8,128)(2,1)}, u32[]{:S(2)}, u32[]{:S(2)}) collective-permute-start(bf16[2,256,768]{2,1,0:T(8,128)(2,1)} %get-tuple-element.165), channel_id=1, source_target_pairs={{0,4},{1,5},{2,6},{3,7},{4,8},{5,9},{6,10},{7,11},{8,12},{9,13},{1... | collective-permute-start | bytes 2359304 | tf_op jit(solution)/shard_map/ppermute | solution.py:60
  183.2 29.1 %collective-permute-start.32 = (bf16[2,2,128,768]{3,2,1,0:T(8,128)(2,1)}, bf16[2,2,128,768]{3,2,1,0:T(8,128)(2,1)}, u32[]{:S(2)}, u32[]{:S(2)}) collective-permute-start(bf16[2,2,128,768]{3,2,1,0:T(8,128)(2,1)} %get-tuple-element.167), channel_id=1, source_target_pairs={{0,1},{1,0},{2,3},{3,2},{4,5},{5,4},{6,7},{7,6},{8,9},{9,8},{10,11... | collective-permute-start | bytes 2359304 | tf_op jit(solution)/shard_map/ppermute | solution.py:60
  184.0 28.3 %collective-permute-start.33 = (bf16[5,128,768]{2,1,0:T(8,128)(2,1)}, bf16[5,128,768]{2,1,0:T(8,128)(2,1)}, u32[]{:S(2)}, u32[]{:S(2)}) collective-permute-start(bf16[5,128,768]{2,1,0:T(8,128)(2,1)} %get-tuple-element.169), channel_id=1, source_target_pairs={{0,12},{1,13},{2,14},{3,15},{4,0},{5,1},{6,2},{7,3},{8,4},{9,5},{1... | collective-permute-start | bytes 2949128 | tf_op jit(solution)/shard_map/ppermute | solution.py:60
  215.1 19.5 %collective-permute-start.38 = (bf16[192,2048]{1,0:T(8,128)(2,1)}, bf16[192,2048]{1,0:T(8,128)(2,1)}, u32[]{:S(2)}, u32[]{:S(2)}) collective-permute-start(bf16[192,2048]{1,0:T(8,128)(2,1)} %bitcast.15), channel_id=1, source_target_pairs={{0,3},{1,2},{2,1},{3,0},{4,7},{5,6},{6,5},{7,4},{8,11},{9,10},{10,... | collective-permute-start | bytes 2359304 | tf_op jit(solution)/shard_map/ppermute | solution.py:60
  224.6 33.5 %all-to-all-start.5 = ((bf16[4,96,2048]{2,1,0:T(8,128)(2,1)}), bf16[4,96,2048]{2,1,0:T(8,128)(2,1)}, u32[]{:S(2)}, u32[]{:S(2)}) async-start(bf16[4,96,2048]{2,1,0:T(8,128)(2,1)} %pad_maximum_fusion), calls=%async_computation.5 | async-start | bytes 3145728 | tf_op jit(solution)/shard_map/all_to_all | solution.py:63
  239.4 29.9 %collective-permute-start.41 = (bf16[192,2048]{1,0:T(8,128)(2,1)}, bf16[192,2048]{1,0:T(8,128)(2,1)S(1)}, u32[]{:S(2)}, u32[]{:S(2)}) collective-permute-start(bf16[192,2048]{1,0:T(8,128)(2,1)} %bitcast.21), channel_id=1, source_target_pairs={{0,3},{1,2},{2,1},{3,0},{4,7},{5,6},{6,5},{7,4},{8,11},{9,10},{10,... | collective-permute-start | bytes 2359304 | tf_op jit(solution)/shard_map/ppermute | solution.py:60
  (81 other events, 794.0 us)
